TPU v7x, 128 devices: a whole 4x4x4 slice. The times are simulated.
128 devices in a mesh: req: 8 (over y, z_lo), ctx: 16 (over x, z_hi, core).
Axes of the slice: x: 4, y: 4, z: 4 (z_hi: 2, z_lo: 2; z = z_hi * 2 + z_lo), core: 2. Of those that a mesh axis runs over, the one named last changes fastest.
Arguments:
- queries: bfloat16 [8, 4096, 4096], P('req', 'ctx'), may hold values from -6 to 6
- kv_new: bfloat16 [8, 2, 4096, 1024], P('req', None, 'ctx'), may hold values from -12 to 12
- kv_pool: bfloat16 [512, 2, 32, 1024], P(('req', 'ctx')), may hold values from -12 to 12
- prefix_pages: int32 [8], P('req'), may hold values from 32 to 64
- reader_owner: int32 [8, 16, 4], P('req', 'ctx'), may hold values from -1 to 7, as said below
- send_page: int32 [8, 16, 8], P('req', 'ctx'), may hold values from -1 to 3, as said below
- tile_doc: int32 [8, 32], P('req'), may hold values from 0 to 8, as said below
Outputs:
- attended: bfloat16 [8, 4096, 4096], P('req', 'ctx')
Inputs may be any that keep to these rules, and one draw needn't show every extreme that they name: reader_owner[g, c, i] is -1 exactly where i * 16 + c >= prefix_pages[g]; the entries that are not -1 in one row [g, c] are different groups. send_page[o, c, g] is -1 exactly where reader_owner[g, c] does not name o, else a page number within device c of group o. tile_doc[g] never falls along the tiles; each document number covers 1 to 16 neighbouring tiles.
All inputs are finite; a program needn't handle non-finite values.
Results may differ from a plain program's by a relative error of at most 0.006.
Values may be sent and summed in bfloat16 or wider, within the bound.
A program may use at most 64 MiB of HBM per device.

v0:
```python
import math

import jax
import jax.numpy as jnp
from jax import lax
from jax.sharding import PartitionSpec as P

HEAD_SIZE = 128
TILE_POSITIONS = 128


neg_fill = -1e30


def shifted(value, axis, steps):
    count = lax.axis_size(axis)
    pairs = [(source, (source + steps) % count) for source in range(count)]
    return lax.ppermute(value, axis, pairs)


def local(queries, kv_new, kv_pool, prefix_pages, reader_owner, send_page, tile_doc):
    columns = lax.axis_size("ctx")
    own_index = lax.axis_index("ctx")
    row_count = queries.shape[1]
    kv_width = kv_new.shape[3]
    kv_heads = kv_width // HEAD_SIZE
    group_size = queries.shape[2] // HEAD_SIZE // kv_heads
    page_len = kv_pool.shape[2]
    slot_count = reader_owner.shape[2]
    score_scale = 1.0 / math.sqrt(HEAD_SIZE)
    wanted = send_page[0, 0]
    outgoing = jnp.take(kv_pool, jnp.maximum(wanted, 0), axis=0)
    outgoing = jnp.where((wanted >= 0)[:, None, None, None], outgoing, jnp.zeros_like(outgoing))
    arrived = lax.all_to_all(outgoing, "req", split_axis=0, concat_axis=0, tiled=True)
    owners = reader_owner[0, 0]
    prefix_kv = jnp.take(arrived, jnp.maximum(owners, 0), axis=0)
    prefix_kv = jnp.transpose(prefix_kv, (1, 0, 2, 3)).reshape(2, slot_count * page_len, kv_width)
    local_block = jnp.concatenate([kv_new[0], prefix_kv], axis=1)
    prefix_length = prefix_pages[0]
    doc_tokens = jnp.repeat(tile_doc[0], TILE_POSITIONS)
    query_pos = own_index * row_count + jnp.arange(row_count, dtype=jnp.int32)
    query_doc = lax.dynamic_slice_in_dim(doc_tokens, own_index * row_count, row_count)
    query_head_rows = queries[0].reshape(row_count, kv_heads, group_size, HEAD_SIZE)

    def visibility(source):
        key_pos = source * row_count + jnp.arange(row_count, dtype=jnp.int32)
        key_doc = lax.dynamic_slice_in_dim(doc_tokens, source * row_count, row_count)
        new_visible = (key_pos[None, :] <= query_pos[:, None]) & (
            key_doc[None, :] == query_doc[:, None]
        )
        page_live = jnp.arange(slot_count, dtype=jnp.int32) * columns + source < prefix_length
        prefix_visible = jnp.broadcast_to(
            jnp.repeat(page_live, page_len)[None, :], (row_count, slot_count * page_len)
        )
        return (new_visible, prefix_visible)

    def update(current, query_part, key_rows, value_rows, visible):
        running_max, denominator, weighted = current
        scores = (
            jnp.einsum("qhgd,khd->hgqk", query_part, key_rows, preferred_element_type=jnp.float32)
            * score_scale
        )
        scores = jnp.where(visible, scores, -jnp.inf)
        new_max = jnp.maximum(running_max, jnp.max(scores, axis=-1))
        weights = jnp.where(visible, jnp.exp(scores - new_max[..., None]), 0.0)
        rescale = jnp.exp(running_max - new_max)
        denominator = denominator * rescale + jnp.sum(weights, axis=-1)
        rounded = weights.astype(jnp.bfloat16)
        added = jnp.einsum(
            "hgqk,khd->qhgd", rounded, value_rows, preferred_element_type=jnp.float32
        )
        weighted = weighted * jnp.transpose(rescale, (2, 0, 1))[..., None] + added
        return (new_max, denominator, weighted)

    def attend(current, query_part, part_block, source):
        heads_here = part_block.shape[2] // HEAD_SIZE
        key_rows = part_block[0].reshape(part_block.shape[1], heads_here, HEAD_SIZE)
        value_rows = part_block[1].reshape(part_block.shape[1], heads_here, HEAD_SIZE)
        new_visible, prefix_visible = visibility(source)
        visible = jnp.concatenate([new_visible, prefix_visible], axis=1)
        current = update(current, query_part, key_rows, value_rows, visible)
        return current

    state_now = attend(
        (
            jnp.full((kv_heads, group_size, row_count), neg_fill, jnp.float32),
            jnp.zeros((kv_heads, group_size, row_count), jnp.float32),
            jnp.zeros((row_count, kv_heads, group_size, HEAD_SIZE), jnp.float32),
        ),
        query_head_rows,
        local_block,
        own_index,
    )

    def advance(turn_index, loop_state):
        travelling, present = loop_state
        travelling = shifted(travelling, "ctx", 1)
        present = attend(present, query_head_rows, travelling, (own_index - turn_index) % columns)
        return (travelling, present)

    state_now = lax.fori_loop(1, columns, advance, (local_block, state_now))[1]
    denominator = state_now[1]
    weighted = state_now[2]
    result = weighted / jnp.transpose(denominator, (2, 0, 1))[..., None]
    return result.reshape(1, row_count, kv_heads * group_size * HEAD_SIZE).astype(jnp.bfloat16)


def solution(mesh):
    in_specs = (
        P("req", "ctx", None),
        P("req", None, "ctx", None),
        P(("req", "ctx"), None, None, None),
        P("req"),
        P("req", "ctx", None),
        P("req", "ctx", None),
        P("req", None),
    )
    out_specs = P("req", "ctx", None)
    return jax.shard_map(local, mesh=mesh, in_specs=in_specs, out_specs=out_specs, check_vma=False)
```

profile of v0, /device:TPU:0, one launch (start us, length us, event | category | flops | bytes accessed | tf_op | source)
XLA Modules:
  0.0 612.5 jit_solution(6914975547434503041)
XLA Ops:
  3.3 5.9 all-to-all-start
  17.5 7.7 %all-to-all-done = bf16[8,2,32,1024]{3,2,1,0:T(8,128)(2,1)} async-done(((bf16[8,2,32,1024]{3,2,1,0:T(8,128)(2,1)}), bf16[8,2,32,1024]{3,2,1,0:T(8,128)(2,1)}, u32[]{:S(2)}, u32[]{:S(2)}) %all-to-all-start) | async-done | bytes 1048608 | tf_op jit(solution)/shard_map/all_to_all | solution.py:34
  43.5 5.3 copy.48
  48.9 556.3 %while.22 = (s32[]{:T(128)}, bf16[2,384,1024]{1,2,0:T(8,128)(2,1)}, f32[8,4,256]{2,1,0:T(4,128)S(1)}, f32[8,4,256]{2,1,0:T(4,128)S(1)}, f32[256,8,4,128]{3,0,2,1...) while((s32[]{:T(128)}, bf16[2,384,1024]{1,2,0:T(8,128)(2,1)}, ...), condition=%wide.region_5.6_spmd.clone, body=%wide.region_2.5_spmd.clone.sunk | while | flops 1653924352 | bytes 105391840 | solution.py:101
  50.0 22.5 %collective-permute-done = bf16[2,384,1024]{1,2,0:T(8,128)(2,1)S(1)} collective-permute-done((bf16[2,384,1024]{1,2,0:T(8,128)(2,1)}, bf16[2,384,1024]{1,2,0:T(8,128)(2,1)S(1)}, u32[]{:S(2)}, u32[]{:S(2)}) %collective-permute-start) | collective-permute-done | bytes 1572896 | tf_op jit(solution)/shard_map/while/body/eval_jaxpr/ppermute | solution.py:18
  78.4 5.1 bitcast_add_fusion.3
  87.1 22.5 %collective-permute-done = bf16[2,384,1024]{1,2,0:T(8,128)(2,1)S(1)} collective-permute-done((bf16[2,384,1024]{1,2,0:T(8,128)(2,1)}, bf16[2,384,1024]{1,2,0:T(8,128)(2,1)S(1)}, u32[]{:S(2)}, u32[]{:S(2)}) %collective-permute-start) | collective-permute-done | bytes 1572896 | tf_op jit(solution)/shard_map/while/body/eval_jaxpr/ppermute | solution.py:18
  124.2 22.5 %collective-permute-done = bf16[2,384,1024]{1,2,0:T(8,128)(2,1)S(1)} collective-permute-done((bf16[2,384,1024]{1,2,0:T(8,128)(2,1)}, bf16[2,384,1024]{1,2,0:T(8,128)(2,1)S(1)}, u32[]{:S(2)}, u32[]{:S(2)}) %collective-permute-start) | collective-permute-done | bytes 1572896 | tf_op jit(solution)/shard_map/while/body/eval_jaxpr/ppermute | solution.py:18
  152.6 5.1 bitcast_add_fusion.3
  161.3 22.5 %collective-permute-done = bf16[2,384,1024]{1,2,0:T(8,128)(2,1)S(1)} collective-permute-done((bf16[2,384,1024]{1,2,0:T(8,128)(2,1)}, bf16[2,384,1024]{1,2,0:T(8,128)(2,1)S(1)}, u32[]{:S(2)}, u32[]{:S(2)}) %collective-permute-start) | collective-permute-done | bytes 1572896 | tf_op jit(solution)/shard_map/while/body/eval_jaxpr/ppermute | solution.py:18
  189.7 5.1 bitcast_add_fusion.3
  198.4 22.5 %collective-permute-done = bf16[2,384,1024]{1,2,0:T(8,128)(2,1)S(1)} collective-permute-done((bf16[2,384,1024]{1,2,0:T(8,128)(2,1)}, bf16[2,384,1024]{1,2,0:T(8,128)(2,1)S(1)}, u32[]{:S(2)}, u32[]{:S(2)}) %collective-permute-start) | collective-permute-done | bytes 1572896 | tf_op jit(solution)/shard_map/while/body/eval_jaxpr/ppermute | solution.py:18
  226.8 5.1 bitcast_add_fusion.3
  235.5 22.5 %collective-permute-done = bf16[2,384,1024]{1,2,0:T(8,128)(2,1)S(1)} collective-permute-done((bf16[2,384,1024]{1,2,0:T(8,128)(2,1)}, bf16[2,384,1024]{1,2,0:T(8,128)(2,1)S(1)}, u32[]{:S(2)}, u32[]{:S(2)}) %collective-permute-start) | collective-permute-done | bytes 1572896 | tf_op jit(solution)/shard_map/while/body/eval_jaxpr/ppermute | solution.py:18
  272.6 22.5 %collective-permute-done = bf16[2,384,1024]{1,2,0:T(8,128)(2,1)S(1)} collective-permute-done((bf16[2,384,1024]{1,2,0:T(8,128)(2,1)}, bf16[2,384,1024]{1,2,0:T(8,128)(2,1)S(1)}, u32[]{:S(2)}, u32[]{:S(2)}) %collective-permute-start) | collective-permute-done | bytes 1572896 | tf_op jit(solution)/shard_map/while/body/eval_jaxpr/ppermute | solution.py:18
  300.9 5.1 bitcast_add_fusion.3
  309.7 22.5 %collective-permute-done = bf16[2,384,1024]{1,2,0:T(8,128)(2,1)S(1)} collective-permute-done((bf16[2,384,1024]{1,2,0:T(8,128)(2,1)}, bf16[2,384,1024]{1,2,0:T(8,128)(2,1)S(1)}, u32[]{:S(2)}, u32[]{:S(2)}) %collective-permute-start) | collective-permute-done | bytes 1572896 | tf_op jit(solution)/shard_map/while/body/eval_jaxpr/ppermute | solution.py:18
  346.7 22.5 %collective-permute-done = bf16[2,384,1024]{1,2,0:T(8,128)(2,1)S(1)} collective-permute-done((bf16[2,384,1024]{1,2,0:T(8,128)(2,1)}, bf16[2,384,1024]{1,2,0:T(8,128)(2,1)S(1)}, u32[]{:S(2)}, u32[]{:S(2)}) %collective-permute-start) | collective-permute-done | bytes 1572896 | tf_op jit(solution)/shard_map/while/body/eval_jaxpr/ppermute | solution.py:18
  383.8 22.5 %collective-permute-done = bf16[2,384,1024]{1,2,0:T(8,128)(2,1)S(1)} collective-permute-done((bf16[2,384,1024]{1,2,0:T(8,128)(2,1)}, bf16[2,384,1024]{1,2,0:T(8,128)(2,1)S(1)}, u32[]{:S(2)}, u32[]{:S(2)}) %collective-permute-start) | collective-permute-done | bytes 1572896 | tf_op jit(solution)/shard_map/while/body/eval_jaxpr/ppermute | solution.py:18
  420.9 22.5 %collective-permute-done = bf16[2,384,1024]{1,2,0:T(8,128)(2,1)S(1)} collective-permute-done((bf16[2,384,1024]{1,2,0:T(8,128)(2,1)}, bf16[2,384,1024]{1,2,0:T(8,128)(2,1)S(1)}, u32[]{:S(2)}, u32[]{:S(2)}) %collective-permute-start) | collective-permute-done | bytes 1572896 | tf_op jit(solution)/shard_map/while/body/eval_jaxpr/ppermute | solution.py:18
  458.0 22.5 %collective-permute-done = bf16[2,384,1024]{1,2,0:T(8,128)(2,1)S(1)} collective-permute-done((bf16[2,384,1024]{1,2,0:T(8,128)(2,1)}, bf16[2,384,1024]{1,2,0:T(8,128)(2,1)S(1)}, u32[]{:S(2)}, u32[]{:S(2)}) %collective-permute-start) | collective-permute-done | bytes 1572896 | tf_op jit(solution)/shard_map/while/body/eval_jaxpr/ppermute | solution.py:18
  495.1 22.5 %collective-permute-done = bf16[2,384,1024]{1,2,0:T(8,128)(2,1)S(1)} collective-permute-done((bf16[2,384,1024]{1,2,0:T(8,128)(2,1)}, bf16[2,384,1024]{1,2,0:T(8,128)(2,1)S(1)}, u32[]{:S(2)}, u32[]{:S(2)}) %collective-permute-start) | collective-permute-done | bytes 1572896 | tf_op jit(solution)/shard_map/while/body/eval_jaxpr/ppermute | solution.py:18
  532.2 22.5 %collective-permute-done = bf16[2,384,1024]{1,2,0:T(8,128)(2,1)S(1)} collective-permute-done((bf16[2,384,1024]{1,2,0:T(8,128)(2,1)}, bf16[2,384,1024]{1,2,0:T(8,128)(2,1)S(1)}, u32[]{:S(2)}, u32[]{:S(2)}) %collective-permute-start) | collective-permute-done | bytes 1572896 | tf_op jit(solution)/shard_map/while/body/eval_jaxpr/ppermute | solution.py:18
  569.3 22.5 %collective-permute-done = bf16[2,384,1024]{1,2,0:T(8,128)(2,1)S(1)} collective-permute-done((bf16[2,384,1024]{1,2,0:T(8,128)(2,1)}, bf16[2,384,1024]{1,2,0:T(8,128)(2,1)S(1)}, u32[]{:S(2)}, u32[]{:S(2)}) %collective-permute-start) | collective-permute-done | bytes 1572896 | tf_op jit(solution)/shard_map/while/body/eval_jaxpr/ppermute | solution.py:18
  (397 shorter events, 228.7 us)
Async XLA Ops:
  3.3 21.9 %all-to-all-start = ((bf16[8,2,32,1024]{3,2,1,0:T(8,128)(2,1)}), bf16[8,2,32,1024]{3,2,1,0:T(8,128)(2,1)}, u32[]{:S(2)}, u32[]{:S(2)}) async-start(bf16[8,2,32,1024]{3,2,1,0:T(8,128)(2,1)} %select_select_fusion), calls=%async_computation | async-start | bytes 2097152 | tf_op jit(solution)/shard_map/all_to_all | solution.py:34
  48.9 23.7 %collective-permute-start = (bf16[2,384,1024]{1,2,0:T(8,128)(2,1)}, bf16[2,384,1024]{1,2,0:T(8,128)(2,1)S(1)}, u32[]{:S(2)}, u32[]{:S(2)}) collective-permute-start(bf16[2,384,1024]{1,2,0:T(8,128)(2,1)} %get-tuple-element.476), channel_id=1, source_target_pairs={{0,1},{1,2},{2,3},{3,4},{4,5},{5,6},{6,7},{7,8},{8,9},{9,10},{10,1... | collective-permute-start | bytes 4718600 | tf_op jit(solution)/shard_map/while/body/eval_jaxpr/ppermute | solution.py:18
  49.7 23.0 %copy-start.1 = (bf16[256,8,4,128]{3,0,2,1:T(8,128)(2,1)S(1)}, bf16[256,8,4,128]{3,0,2,1:T(8,128)(2,1)}, u32[]{:S(2)}) copy-start(bf16[256,8,4,128]{3,0,2,1:T(8,128)(2,1)} %get-tuple-element.502) | copy-start | bytes 6291460 | tf_op jit(solution)/shard_map/while
  85.9 23.7 %collective-permute-start = (bf16[2,384,1024]{1,2,0:T(8,128)(2,1)}, bf16[2,384,1024]{1,2,0:T(8,128)(2,1)S(1)}, u32[]{:S(2)}, u32[]{:S(2)}) collective-permute-start(bf16[2,384,1024]{1,2,0:T(8,128)(2,1)} %get-tuple-element.476), channel_id=1, source_target_pairs={{0,1},{1,2},{2,3},{3,4},{4,5},{5,6},{6,7},{7,8},{8,9},{9,10},{10,1... | collective-permute-start | bytes 4718600 | tf_op jit(solution)/shard_map/while/body/eval_jaxpr/ppermute | solution.py:18
  86.8 23.0 %copy-start.1 = (bf16[256,8,4,128]{3,0,2,1:T(8,128)(2,1)S(1)}, bf16[256,8,4,128]{3,0,2,1:T(8,128)(2,1)}, u32[]{:S(2)}) copy-start(bf16[256,8,4,128]{3,0,2,1:T(8,128)(2,1)} %get-tuple-element.502) | copy-start | bytes 6291460 | tf_op jit(solution)/shard_map/while
  123.0 23.7 %collective-permute-start = (bf16[2,384,1024]{1,2,0:T(8,128)(2,1)}, bf16[2,384,1024]{1,2,0:T(8,128)(2,1)S(1)}, u32[]{:S(2)}, u32[]{:S(2)}) collective-permute-start(bf16[2,384,1024]{1,2,0:T(8,128)(2,1)} %get-tuple-element.476), channel_id=1, source_target_pairs={{0,1},{1,2},{2,3},{3,4},{4,5},{5,6},{6,7},{7,8},{8,9},{9,10},{10,1... | collective-permute-start | bytes 4718600 | tf_op jit(solution)/shard_map/while/body/eval_jaxpr/ppermute | solution.py:18
  123.8 23.0 %copy-start.1 = (bf16[256,8,4,128]{3,0,2,1:T(8,128)(2,1)S(1)}, bf16[256,8,4,128]{3,0,2,1:T(8,128)(2,1)}, u32[]{:S(2)}) copy-start(bf16[256,8,4,128]{3,0,2,1:T(8,128)(2,1)} %get-tuple-element.502) | copy-start | bytes 6291460 | tf_op jit(solution)/shard_map/while
  160.1 23.7 %collective-permute-start = (bf16[2,384,1024]{1,2,0:T(8,128)(2,1)}, bf16[2,384,1024]{1,2,0:T(8,128)(2,1)S(1)}, u32[]{:S(2)}, u32[]{:S(2)}) collective-permute-start(bf16[2,384,1024]{1,2,0:T(8,128)(2,1)} %get-tuple-element.476), channel_id=1, source_target_pairs={{0,1},{1,2},{2,3},{3,4},{4,5},{5,6},{6,7},{7,8},{8,9},{9,10},{10,1... | collective-permute-start | bytes 4718600 | tf_op jit(solution)/shard_map/while/body/eval_jaxpr/ppermute | solution.py:18
  160.9 23.0 %copy-start.1 = (bf16[256,8,4,128]{3,0,2,1:T(8,128)(2,1)S(1)}, bf16[256,8,4,128]{3,0,2,1:T(8,128)(2,1)}, u32[]{:S(2)}) copy-start(bf16[256,8,4,128]{3,0,2,1:T(8,128)(2,1)} %get-tuple-element.502) | copy-start | bytes 6291460 | tf_op jit(solution)/shard_map/while
  197.2 23.7 %collective-permute-start = (bf16[2,384,1024]{1,2,0:T(8,128)(2,1)}, bf16[2,384,1024]{1,2,0:T(8,128)(2,1)S(1)}, u32[]{:S(2)}, u32[]{:S(2)}) collective-permute-start(bf16[2,384,1024]{1,2,0:T(8,128)(2,1)} %get-tuple-element.476), channel_id=1, source_target_pairs={{0,1},{1,2},{2,3},{3,4},{4,5},{5,6},{6,7},{7,8},{8,9},{9,10},{10,1... | collective-permute-start | bytes 4718600 | tf_op jit(solution)/shard_map/while/body/eval_jaxpr/ppermute | solution.py:18
  198.0 23.0 %copy-start.1 = (bf16[256,8,4,128]{3,0,2,1:T(8,128)(2,1)S(1)}, bf16[256,8,4,128]{3,0,2,1:T(8,128)(2,1)}, u32[]{:S(2)}) copy-start(bf16[256,8,4,128]{3,0,2,1:T(8,128)(2,1)} %get-tuple-element.502) | copy-start | bytes 6291460 | tf_op jit(solution)/shard_map/while
  234.3 23.7 %collective-permute-start = (bf16[2,384,1024]{1,2,0:T(8,128)(2,1)}, bf16[2,384,1024]{1,2,0:T(8,128)(2,1)S(1)}, u32[]{:S(2)}, u32[]{:S(2)}) collective-permute-start(bf16[2,384,1024]{1,2,0:T(8,128)(2,1)} %get-tuple-element.476), channel_id=1, source_target_pairs={{0,1},{1,2},{2,3},{3,4},{4,5},{5,6},{6,7},{7,8},{8,9},{9,10},{10,1... | collective-permute-start | bytes 4718600 | tf_op jit(solution)/shard_map/while/body/eval_jaxpr/ppermute | solution.py:18
  235.1 23.0 %copy-start.1 = (bf16[256,8,4,128]{3,0,2,1:T(8,128)(2,1)S(1)}, bf16[256,8,4,128]{3,0,2,1:T(8,128)(2,1)}, u32[]{:S(2)}) copy-start(bf16[256,8,4,128]{3,0,2,1:T(8,128)(2,1)} %get-tuple-element.502) | copy-start | bytes 6291460 | tf_op jit(solution)/shard_map/while
  271.4 23.7 %collective-permute-start = (bf16[2,384,1024]{1,2,0:T(8,128)(2,1)}, bf16[2,384,1024]{1,2,0:T(8,128)(2,1)S(1)}, u32[]{:S(2)}, u32[]{:S(2)}) collective-permute-start(bf16[2,384,1024]{1,2,0:T(8,128)(2,1)} %get-tuple-element.476), channel_id=1, source_target_pairs={{0,1},{1,2},{2,3},{3,4},{4,5},{5,6},{6,7},{7,8},{8,9},{9,10},{10,1... | collective-permute-start | bytes 4718600 | tf_op jit(solution)/shard_map/while/body/eval_jaxpr/ppermute | solution.py:18
  272.2 23.0 %copy-start.1 = (bf16[256,8,4,128]{3,0,2,1:T(8,128)(2,1)S(1)}, bf16[256,8,4,128]{3,0,2,1:T(8,128)(2,1)}, u32[]{:S(2)}) copy-start(bf16[256,8,4,128]{3,0,2,1:T(8,128)(2,1)} %get-tuple-element.502) | copy-start | bytes 6291460 | tf_op jit(solution)/shard_map/while
  308.5 23.7 %collective-permute-start = (bf16[2,384,1024]{1,2,0:T(8,128)(2,1)}, bf16[2,384,1024]{1,2,0:T(8,128)(2,1)S(1)}, u32[]{:S(2)}, u32[]{:S(2)}) collective-permute-start(bf16[2,384,1024]{1,2,0:T(8,128)(2,1)} %get-tuple-element.476), channel_id=1, source_target_pairs={{0,1},{1,2},{2,3},{3,4},{4,5},{5,6},{6,7},{7,8},{8,9},{9,10},{10,1... | collective-permute-start | bytes 4718600 | tf_op jit(solution)/shard_map/while/body/eval_jaxpr/ppermute | solution.py:18
  309.3 23.0 %copy-start.1 = (bf16[256,8,4,128]{3,0,2,1:T(8,128)(2,1)S(1)}, bf16[256,8,4,128]{3,0,2,1:T(8,128)(2,1)}, u32[]{:S(2)}) copy-start(bf16[256,8,4,128]{3,0,2,1:T(8,128)(2,1)} %get-tuple-element.502) | copy-start | bytes 6291460 | tf_op jit(solution)/shard_map/while
  345.6 23.7 %collective-permute-start = (bf16[2,384,1024]{1,2,0:T(8,128)(2,1)}, bf16[2,384,1024]{1,2,0:T(8,128)(2,1)S(1)}, u32[]{:S(2)}, u32[]{:S(2)}) collective-permute-start(bf16[2,384,1024]{1,2,0:T(8,128)(2,1)} %get-tuple-element.476), channel_id=1, source_target_pairs={{0,1},{1,2},{2,3},{3,4},{4,5},{5,6},{6,7},{7,8},{8,9},{9,10},{10,1... | collective-permute-start | bytes 4718600 | tf_op jit(solution)/shard_map/while/body/eval_jaxpr/ppermute | solution.py:18
  382.6 23.7 %collective-permute-start = (bf16[2,384,1024]{1,2,0:T(8,128)(2,1)}, bf16[2,384,1024]{1,2,0:T(8,128)(2,1)S(1)}, u32[]{:S(2)}, u32[]{:S(2)}) collective-permute-start(bf16[2,384,1024]{1,2,0:T(8,128)(2,1)} %get-tuple-element.476), channel_id=1, source_target_pairs={{0,1},{1,2},{2,3},{3,4},{4,5},{5,6},{6,7},{7,8},{8,9},{9,10},{10,1... | collective-permute-start | bytes 4718600 | tf_op jit(solution)/shard_map/while/body/eval_jaxpr/ppermute | solution.py:18
  419.7 23.7 %collective-permute-start = (bf16[2,384,1024]{1,2,0:T(8,128)(2,1)}, bf16[2,384,1024]{1,2,0:T(8,128)(2,1)S(1)}, u32[]{:S(2)}, u32[]{:S(2)}) collective-permute-start(bf16[2,384,1024]{1,2,0:T(8,128)(2,1)} %get-tuple-element.476), channel_id=1, source_target_pairs={{0,1},{1,2},{2,3},{3,4},{4,5},{5,6},{6,7},{7,8},{8,9},{9,10},{10,1... | collective-permute-start | bytes 4718600 | tf_op jit(solution)/shard_map/while/body/eval_jaxpr/ppermute | solution.py:18
  456.8 23.7 %collective-permute-start = (bf16[2,384,1024]{1,2,0:T(8,128)(2,1)}, bf16[2,384,1024]{1,2,0:T(8,128)(2,1)S(1)}, u32[]{:S(2)}, u32[]{:S(2)}) collective-permute-start(bf16[2,384,1024]{1,2,0:T(8,128)(2,1)} %get-tuple-element.476), channel_id=1, source_target_pairs={{0,1},{1,2},{2,3},{3,4},{4,5},{5,6},{6,7},{7,8},{8,9},{9,10},{10,1... | collective-permute-start | bytes 4718600 | tf_op jit(solution)/shard_map/while/body/eval_jaxpr/ppermute | solution.py:18
  493.9 23.7 %collective-permute-start = (bf16[2,384,1024]{1,2,0:T(8,128)(2,1)}, bf16[2,384,1024]{1,2,0:T(8,128)(2,1)S(1)}, u32[]{:S(2)}, u32[]{:S(2)}) collective-permute-start(bf16[2,384,1024]{1,2,0:T(8,128)(2,1)} %get-tuple-element.476), channel_id=1, source_target_pairs={{0,1},{1,2},{2,3},{3,4},{4,5},{5,6},{6,7},{7,8},{8,9},{9,10},{10,1... | collective-permute-start | bytes 4718600 | tf_op jit(solution)/shard_map/while/body/eval_jaxpr/ppermute | solution.py:18
  531.0 23.7 %collective-permute-start = (bf16[2,384,1024]{1,2,0:T(8,128)(2,1)}, bf16[2,384,1024]{1,2,0:T(8,128)(2,1)S(1)}, u32[]{:S(2)}, u32[]{:S(2)}) collective-permute-start(bf16[2,384,1024]{1,2,0:T(8,128)(2,1)} %get-tuple-element.476), channel_id=1, source_target_pairs={{0,1},{1,2},{2,3},{3,4},{4,5},{5,6},{6,7},{7,8},{8,9},{9,10},{10,1... | collective-permute-start | bytes 4718600 | tf_op jit(solution)/shard_map/while/body/eval_jaxpr/ppermute | solution.py:18
  568.1 23.7 %collective-permute-start = (bf16[2,384,1024]{1,2,0:T(8,128)(2,1)}, bf16[2,384,1024]{1,2,0:T(8,128)(2,1)S(1)}, u32[]{:S(2)}, u32[]{:S(2)}) collective-permute-start(bf16[2,384,1024]{1,2,0:T(8,128)(2,1)} %get-tuple-element.476), channel_id=1, source_target_pairs={{0,1},{1,2},{2,3},{3,4},{4,5},{5,6},{6,7},{7,8},{8,9},{9,10},{10,1... | collective-permute-start | bytes 4718600 | tf_op jit(solution)/shard_map/while/body/eval_jaxpr/ppermute | solution.py:18
  (41 other events, 277.0 us)
where the time goes:
time: 613 us; the launch traced here: 612 us
  waiting for transfers between devices  345 us (56%)
  matrix products  120 us (20%)
  other arithmetic  74.9 us (12%)
  local copies, waits for them, and re-layouts  64.6 us (11%)
    ppermute x15, waiting for transfers between devices, shifted(): return lax.ppermute(value, axis, pairs)  337 us
    dot_general x16, matrix products, update(): jnp.einsum('hgqk,khd->qhgd', rounded, value_rows, preferred_element_type=...  81 us
    reduce_sum x16, other arithmetic, update(): denominator = denominator * rescale + jnp.sum(weights, axis=-1)  50.6 us
    dot_general x16, matrix products, update(): jnp.einsum('qhgd,khd->hgqk', query_part, key_rows, preferred_element_type...  38.8 us
    while x120, local copies, waits for them, and re-layouts  37 us
    unnamed x12, local copies, waits for them, and re-layouts  12.3 us
  transfers between devices with their start and end apart: 16, of which 16 were waited for; matrix products, arithmetic and copies ran while one was open for 4% of the time, Pallas kernels for 0%

commit v1 on v0

v1 whole, which is shorter than its diff:
```python
import functools
import math

import jax
import jax.numpy as jnp
from jax import lax
from jax.experimental import pallas as pl
from jax.experimental.pallas import tpu as pltpu
from jax.sharding import PartitionSpec as P

HEAD = 128
TILE = 128
QROWS = 256
CHUNK = 512
FILL = -1e30
SCALE = math.log2(math.e) / math.sqrt(HEAD)


def scores_of(queries, keys):
    return lax.dot_general(
        queries, keys, (((1,), (1,)), ((), ())), preferred_element_type=jnp.float32
    )


def attend_kernel(info, q_ref, new_ref, pre_ref, out_ref):
    block = pl.program_id(0)
    pages = info[0]
    heads = q_ref.shape[1] // HEAD
    rows = heads * QROWS
    page_rows = pre_ref.shape[1] // 64
    queries = jnp.concatenate(
        [q_ref[:, h * HEAD : (h + 1) * HEAD] for h in range(heads)], axis=0
    )

    def fold(state, scores, values):
        top, total, acc = state
        new_top = jnp.maximum(top, jnp.max(scores, axis=1, keepdims=True))
        weights = jnp.exp2((scores - new_top) * SCALE)
        rescale = jnp.exp2((top - new_top) * SCALE)
        total = total * rescale + jnp.sum(weights, axis=1, keepdims=True)
        acc = acc * rescale + jnp.dot(
            weights.astype(jnp.bfloat16), values, preferred_element_type=jnp.float32
        )
        return new_top, total, acc

    first = 32 * page_rows
    scores = scores_of(queries, pre_ref[0, :first, :])
    top = jnp.max(scores, axis=1, keepdims=True)
    weights = jnp.exp2((scores - top) * SCALE)
    total = jnp.sum(weights, axis=1, keepdims=True)
    acc = jnp.dot(
        weights.astype(jnp.bfloat16), pre_ref[1, :first, :], preferred_element_type=jnp.float32
    )
    state = (top, total, acc)

    def prefix_step(i, state):
        at = pl.multiple_of(i * CHUNK, CHUNK)
        scores = scores_of(queries, pre_ref[0, pl.ds(at, CHUNK), :])
        column = lax.broadcasted_iota(jnp.int32, scores.shape, 1)
        scores = jnp.where(column < pages * page_rows - at, scores, FILL)
        return fold(state, scores, pre_ref[1, pl.ds(at, CHUNK), :])

    live = pages * page_rows
    state = lax.fori_loop(first // CHUNK, (live + CHUNK - 1) // CHUNK, prefix_step, state)

    per = QROWS // TILE
    row = lax.broadcasted_iota(jnp.int32, (rows, 1), 0) % QROWS
    low = jnp.full((rows, 1), info[1 + block * per] * TILE, jnp.int32)
    for t in range(1, per):
        low = jnp.where(row >= t * TILE, info[1 + block * per + t] * TILE, low)
    position = row + block * QROWS

    def new_step(i, state):
        at = pl.multiple_of(i * QROWS, QROWS)
        scores = scores_of(queries, new_ref[0, pl.ds(at, QROWS), :])
        column = lax.broadcasted_iota(jnp.int32, scores.shape, 1) + at
        scores = jnp.where((column >= low) & (column <= position), scores, FILL)
        return fold(state, scores, new_ref[1, pl.ds(at, QROWS), :])

    state = lax.fori_loop(info[1 + block * per] // per, block + 1, new_step, state)
    _, total, acc = state
    result = (acc / total).astype(out_ref.dtype)
    for h in range(heads):
        out_ref[:, h * HEAD : (h + 1) * HEAD] = result[h * QROWS : (h + 1) * QROWS]


def attend(info, queries, new_kv, prefix_kv):
    positions, width = queries.shape
    whole = lambda shape: pl.BlockSpec(shape, lambda i, s: (0,) * len(shape))
    return pl.pallas_call(
        attend_kernel,
        out_shape=jax.ShapeDtypeStruct((positions, width), queries.dtype),
        grid_spec=pltpu.PrefetchScalarGridSpec(
            num_scalar_prefetch=1,
            grid=(positions // QROWS,),
            in_specs=[
                pl.BlockSpec((QROWS, width), lambda i, s: (i, 0)),
                whole(new_kv.shape),
                whole(prefix_kv.shape),
            ],
            out_specs=pl.BlockSpec((QROWS, width), lambda i, s: (i, 0)),
        ),
        compiler_params=pltpu.CompilerParams(
            dimension_semantics=("arbitrary",), vmem_limit_bytes=48 << 20
        ),
        cost_estimate=pl.CostEstimate(
            flops=4 * positions * width * 2560, bytes_accessed=10 << 20, transcendentals=0
        ),
        name="attend",
    )(info, queries, new_kv, prefix_kv)


def pick(pages, ids):
    return jnp.stack(
        [
            lax.dynamic_index_in_dim(pages, jnp.maximum(ids[i], 0), 0, keepdims=False)
            for i in range(ids.shape[0])
        ]
    )


def local(queries, kv_new, kv_pool, prefix_pages, reader_owner, send_page, tile_doc):
    columns = lax.axis_size("ctx")
    kv_heads = kv_new.shape[3] // HEAD
    page_len = kv_pool.shape[2]
    slots = reader_owner.shape[2]
    copies = columns // kv_heads
    wanted = send_page[0, 0]
    outgoing = pick(kv_pool, wanted)
    arrived = lax.all_to_all(outgoing, "req", split_axis=0, concat_axis=0, tiled=True)
    prefix_kv = pick(arrived, reader_owner[0, 0])
    prefix_kv = jnp.transpose(prefix_kv, (1, 0, 2, 3)).reshape(2, slots * page_len, -1)
    block = jnp.concatenate([kv_new[0], prefix_kv], axis=1)
    block = block.reshape(2, -1, kv_heads, HEAD)
    block = jnp.repeat(jnp.transpose(block, (2, 0, 1, 3)), copies, axis=0)
    kv = lax.all_to_all(block, "ctx", split_axis=0, concat_axis=0, tiled=True)
    rows = kv_new.shape[2]
    new_kv = jnp.transpose(kv[:, :, :rows], (1, 0, 2, 3)).reshape(2, -1, HEAD)
    pre = kv[:, :, rows:].reshape(columns, 2, slots, page_len, HEAD)
    pre = jnp.transpose(pre, (1, 2, 0, 3, 4)).reshape(2, -1, HEAD)
    q = lax.all_to_all(queries[0], "ctx", split_axis=1, concat_axis=0, tiled=True)
    docs = tile_doc[0]
    starts = jnp.sum((docs[None, :] < docs[:, None]).astype(jnp.int32), axis=1)
    info = jnp.concatenate([prefix_pages, starts])
    out = attend(info, q, new_kv, pre)
    out = lax.all_to_all(out, "ctx", split_axis=0, concat_axis=1, tiled=True)
    return out[None]


def solution(mesh):
    in_specs = (
        P("req", "ctx", None),
        P("req", None, "ctx", None),
        P(("req", "ctx"), None, None, None),
        P("req"),
        P("req", "ctx", None),
        P("req", "ctx", None),
        P("req", None),
    )
    return jax.shard_map(
        local, mesh=mesh, in_specs=in_specs, out_specs=P("req", "ctx", None), check_vma=False
    )
```

time: 613 us -> 254 us (0.41)
  the two profiles are of different devices: /device:TPU:0 before, /device:TPU:10 now
where the time goes in v1:
time: 254 us; the launch traced here: 251 us
  Pallas kernels  84.8 us (33%)
  waiting for transfers between devices  67.6 us (27%)
  blocking collectives  33.1 us (13%)
  local copies, waits for them, and re-layouts  32.1 us (13%)
  starting transfers between devices  24.5 us (10%)
  between operations  8.34 us (3%)
    pallas_call x1, Pallas kernels, attend(): pl.pallas_call(attend_kernel, out_shape=jax.ShapeDtypeStruct((positions,...  84.8 us
    all_to_all x1, waiting for transfers between devices, local(): kv = lax.all_to_all(block, 'ctx', split_axis=0, concat_axis=0, tiled=True)  34.6 us
    all_to_all x1, blocking collectives, local(): out = lax.all_to_all(out, 'ctx', split_axis=0, concat_axis=1, tiled=True)  33.1 us
    all_to_all x1, waiting for transfers between devices, local(): lax.all_to_all(queries[0], 'ctx', split_axis=1, concat_axis=0, tiled=True)  22.1 us
    unnamed x18, local copies, waits for them, and re-layouts  15.3 us
    all_to_all x1, waiting for transfers between devices, local(): lax.all_to_all(outgoing, 'req', split_axis=0, concat_axis=0, tiled=True)  10.9 us
    all_to_all x1, starting transfers between devices, local(): lax.all_to_all(queries[0], 'ctx', split_axis=1, concat_axis=0, tiled=True)  10.3 us
    all_to_all x1, starting transfers between devices, local(): kv = lax.all_to_all(block, 'ctx', split_axis=0, concat_axis=0, tiled=True)  7.87 us
  transfers between devices with their start and end apart: 3, of which 3 were waited for; matrix products, arithmetic and copies ran while one was open for 3% of the time, Pallas kernels for 0%

profile of v1, /device:TPU:10, one launch (start us, length us, event | category | flops | bytes accessed | tf_op | source)
XLA Modules:
  0.0 250.9 jit_solution(11680716799573657539)
XLA Ops:
  0.0 1.6 fusion.1
  6.7 1.7 dynamic-slice_dynamic-update-slice_fusion.7
  8.3 1.6 dynamic-slice_dynamic-update-slice_fusion.6
  9.9 1.6 dynamic-slice_dynamic-update-slice_fusion.5
  11.5 1.6 dynamic-slice_dynamic-update-slice_fusion.4
  13.1 1.6 dynamic-slice_dynamic-update-slice_fusion.3
  14.6 1.6 dynamic-slice_dynamic-update-slice_fusion.2
  16.2 1.6 dynamic-slice_dynamic-update-slice_fusion.1
  17.8 1.6 dynamic-slice_dynamic-update-slice_fusion
  19.3 6.3 %all-to-all-start.1 = ((bf16[8,2,32,1024]{3,2,1,0:T(8,128)(2,1)}), bf16[8,2,32,1024]{3,2,1,0:T(8,128)(2,1)S(1)}, u32[]{:S(2)}, u32[]{:S(2)}) async-start(bf16[8,2,32,1024]{3,2,1,0:T(8,128)(2,1)} %dynamic-slice_dynamic-update-slice_fusion), calls=%async_computation.1 | async-start | bytes 2097152 | tf_op jit(solution)/shard_map/all_to_all | solution.py:130
  29.0 10.9 %all-to-all-done.1 = bf16[8,2,32,1024]{3,2,1,0:T(8,128)(2,1)S(1)} async-done(((bf16[8,2,32,1024]{3,2,1,0:T(8,128)(2,1)}), bf16[8,2,32,1024]{3,2,1,0:T(8,128)(2,1)S(1)}, u32[]{:S(2)}, u32[]{:S(2)}) %all-to-all-start.1) | async-done | bytes 1048608 | tf_op jit(solution)/shard_map/all_to_all | solution.py:130
  40.6 2.5 %broadcast_in_dim.6 = bf16[8,2,2,384,128]{4,3,2,1,0:T(8,128)(2,1)} broadcast(bf16[8,2,384,128]{3,2,1,0:T(8,128)(2,1)S(1)} %copy.19), dimensions={0,2,3,4} | broadcast | bytes 4718592 | tf_op jit(solution)/shard_map/broadcast_in_dim | solution.py:135
  43.2 7.9 %all-to-all-start.2 = ((bf16[16,2,384,128]{3,2,1,0:T(8,128)(2,1)}), bf16[16,2,384,128]{3,2,1,0:T(8,128)(2,1)S(1)}, u32[]{:S(2)}, u32[]{:S(2)}) async-start(bf16[16,2,384,128]{3,2,1,0:T(8,128)(2,1)} %bitcast.47), calls=%async_computation.2 | async-start | bytes 6291456 | tf_op jit(solution)/shard_map/all_to_all | solution.py:136
  51.0 2.2 copy.23
  53.3 2.0 copy.17
  55.3 34.6 %all-to-all-done.2 = bf16[16,2,384,128]{3,2,1,0:T(8,128)(2,1)S(1)} async-done(((bf16[16,2,384,128]{3,2,1,0:T(8,128)(2,1)}), bf16[16,2,384,128]{3,2,1,0:T(8,128)(2,1)S(1)}, u32[]{:S(2)}, u32[]{:S(2)}) %all-to-all-start.2) | async-done | bytes 3145760 | tf_op jit(solution)/shard_map/all_to_all | solution.py:136
  89.9 1.6 copy-done
  91.5 10.3 %all-to-all-start = ((bf16[256,16,256]{2,0,1:T(8,128)(2,1)}), bf16[256,16,256]{2,0,1:T(8,128)(2,1)S(1)}, u32[]{:S(2)}, u32[]{:S(2)}) async-start(bf16[256,16,256]{2,0,1:T(8,128)(2,1)} %copy.17), calls=%async_computation | async-start | bytes 4194304 | tf_op jit(solution)/shard_map/all_to_all | solution.py:141
  102.8 1.7 slice_bitcast_fusion
  104.5 1.5 copy.20
  107.3 22.1 %all-to-all-done = bf16[256,16,256]{2,0,1:T(8,128)(2,1)S(1)} async-done(((bf16[256,16,256]{2,0,1:T(8,128)(2,1)}), bf16[256,16,256]{2,0,1:T(8,128)(2,1)S(1)}, u32[]{:S(2)}, u32[]{:S(2)}) %all-to-all-start) | async-done | bytes 2097184 | tf_op jit(solution)/shard_map/all_to_all | solution.py:141
  129.5 84.8 %attend.1 = bf16[4096,256]{1,0:T(8,128)(2,1)S(1)} custom-call(s32[33]{0:T(128)S(1)} %pad_add_fusion.info, bf16[4096,256]{1,0:T(8,128)(2,1)S(1)} %bitcast.43, bf16[2,4096,128]{2,1,0:T(8,128)(2,1)} %bitcast.52, bf16[2,2048,128]{2,1,0:T(8,128)(2,1)S(1)} %bitcast.45), custom_call_target="tpu_custom_call" | custom-call | flops 10737418240 | bytes 10485760 | tf_op jit(solution)/shard_map/attend/pallas_call | solution.py:90
  214.3 33.1 %all_to_all.45 = bf16[16,256,256]{2,1,0:T(8,128)(2,1)S(1)} all-to-all(bf16[16,256,256]{2,1,0:T(8,128)(2,1)S(1)} %bitcast.44), channel_id=1, replica_groups=mesh['req'=8,'ctx'=16] {'ctx'}, dimensions={0} | all-to-all | bytes 4194304 | tf_op jit(solution)/shard_map/all_to_all | solution.py:146
  248.6 2.3 broadcast_in_dim.7
  (21 shorter events, 4.3 us)
Async XLA Ops:
  6.7 18.9 %copy-start.2 = (s32[1,1,4]{2,1,0:T(1,128)S(1)}, s32[1,1,4]{2,1,0:T(1,128)}, u32[]{:S(2)}) copy-start(s32[1,1,4]{2,1,0:T(1,128)} %param.11) | copy-start | bytes 52
  6.7 22.1 %copy-start.1 = (bf16[1,2,256,1024]{3,2,1,0:T(8,128)(2,1)S(1)}, bf16[1,2,256,1024]{3,2,1,0:T(8,128)(2,1)}, u32[]{:S(2)}) copy-start(bf16[1,2,256,1024]{3,2,1,0:T(8,128)(2,1)} %param.8) | copy-start | bytes 3145732
  19.3 20.6 %all-to-all-start.1 = ((bf16[8,2,32,1024]{3,2,1,0:T(8,128)(2,1)}), bf16[8,2,32,1024]{3,2,1,0:T(8,128)(2,1)S(1)}, u32[]{:S(2)}, u32[]{:S(2)}) async-start(bf16[8,2,32,1024]{3,2,1,0:T(8,128)(2,1)} %dynamic-slice_dynamic-update-slice_fusion), calls=%async_computation.1 | async-start | bytes 2097152 | tf_op jit(solution)/shard_map/all_to_all | solution.py:130
  43.2 46.7 %all-to-all-start.2 = ((bf16[16,2,384,128]{3,2,1,0:T(8,128)(2,1)}), bf16[16,2,384,128]{3,2,1,0:T(8,128)(2,1)S(1)}, u32[]{:S(2)}, u32[]{:S(2)}) async-start(bf16[16,2,384,128]{3,2,1,0:T(8,128)(2,1)} %bitcast.47), calls=%async_computation.2 | async-start | bytes 6291456 | tf_op jit(solution)/shard_map/all_to_all | solution.py:136
  55.3 47.2 %copy-start.3 = (s32[1,32]{1,0:T(1,128)S(1)}, s32[1,32]{1,0:T(1,128)}, u32[]{:S(2)}) copy-start(s32[1,32]{1,0:T(1,128)} %param.13) | copy-start | bytes 388
  89.9 1.6 copy-start
  91.5 38.0 %all-to-all-start = ((bf16[256,16,256]{2,0,1:T(8,128)(2,1)}), bf16[256,16,256]{2,0,1:T(8,128)(2,1)S(1)}, u32[]{:S(2)}, u32[]{:S(2)}) async-start(bf16[256,16,256]{2,0,1:T(8,128)(2,1)} %copy.17), calls=%async_computation | async-start | bytes 4194304 | tf_op jit(solution)/shard_map/all_to_all | solution.py:141
  106.0 1.2 slice-start

commit v2 on v1

v2 whole, which is shorter than its diff:
```python
import math

import jax
import jax.numpy as jnp
from jax import lax
from jax.experimental import pallas as pl
from jax.experimental.pallas import tpu as pltpu
from jax.sharding import PartitionSpec as P

HEAD = 128
TILE = 128
FILL = -1e30
SCALE = math.log2(math.e) / math.sqrt(HEAD)
MESH = pl.DeviceIdType.MESH


def scores_of(queries, keys):
    return lax.dot_general(
        queries, keys, (((1,), (1,)), ((), ())), preferred_element_type=jnp.float32
    )


def decay(scores, top):
    return jnp.exp2((scores - top) * SCALE)


def gather_kernel(
    columns, groups, wanted, owners, pool, q_ref, new_ref, q_all, kv_all, pre_all,
    outgoing, arrived, staged, req_send, req_recv, q_send, q_recv, kv_send, kv_recv,
    kv_pass, pre_send, pre_recv, pre_pass, near,
):
    me = lax.axis_index("ctx")
    group = lax.axis_index("req")
    chips = columns // 2
    chip = me // 2
    core = me % 2
    sibling = chip * 2 + (1 - core)
    rows = q_ref.shape[0]
    width = q_all.shape[1]

    barrier = pltpu.get_barrier_semaphore()

    def greet_column(t, c):
        pl.semaphore_signal(
            barrier, inc=1, device_id={"ctx": (me + t) % columns}, device_id_type=MESH
        )
        return c

    def greet_group(t, c):
        pl.semaphore_signal(
            barrier, inc=1, device_id={"req": (group + t) % groups}, device_id_type=MESH
        )
        return c

    lax.fori_loop(1, columns, greet_column, 0)
    lax.fori_loop(1, groups, greet_group, 0)
    for g in range(groups):
        outgoing[g] = pool[jnp.maximum(wanted[0, 0, g], 0)]
    arrived[group] = outgoing[group]
    pl.semaphore_wait(barrier, columns + groups - 2)

    def page_copy(t):
        to = (group + t) % groups
        return pltpu.make_async_remote_copy(
            outgoing.at[to], arrived.at[group], req_send.at[t], req_recv.at[group],
            device_id={"req": to}, device_id_type=MESH,
        )

    def q_copy(t):
        to = (me + t) % columns
        return pltpu.make_async_remote_copy(
            q_ref.at[:, pl.ds(pl.multiple_of(to * width, width), width)],
            q_all.at[pl.ds(pl.multiple_of(me * rows, rows), rows), :],
            q_send.at[t], q_recv.at[me], device_id={"ctx": to}, device_id_type=MESH,
        )

    def kv_slot(source):
        return kv_all.at[:, pl.ds(pl.multiple_of(source * rows, rows), rows), :]

    def head(ref, at):
        cut = pl.ds(pl.multiple_of(at * HEAD, HEAD), HEAD)
        return ref.at[:, :, cut] if len(ref.shape) == 3 else ref.at[:, :, :, cut]

    def kv_copy(t):
        to = (chip + t) % chips
        return pltpu.make_async_remote_copy(
            head(new_ref, to), kv_slot(me), kv_send.at[t], kv_recv.at[me],
            device_id={"ctx": to * 2 + core}, device_id_type=MESH,
        )

    def pre_copy(t):
        to = (chip + t) % chips
        return pltpu.make_async_remote_copy(
            head(staged, to), pre_all.at[:, :, me], pre_send.at[t], pre_recv.at[me],
            device_id={"ctx": to * 2 + core}, device_id_type=MESH,
        )

    def source_of(t):
        return ((chip + chips - t) % chips) * 2 + core

    def kv_onward(t):
        slot = kv_slot(source_of(t))
        return pltpu.make_async_remote_copy(
            slot, slot, kv_pass.at[t], kv_recv.at[source_of(t)],
            device_id={"ctx": sibling}, device_id_type=MESH,
        )

    def pre_onward(t):
        slot = pre_all.at[:, :, source_of(t)]
        return pltpu.make_async_remote_copy(
            slot, slot, pre_pass.at[t], pre_recv.at[source_of(t)],
            device_id={"ctx": sibling}, device_id_type=MESH,
        )

    def kv_twin():
        return pltpu.make_async_remote_copy(
            head(new_ref, chip), kv_slot(me), kv_pass.at[0], kv_recv.at[me],
            device_id={"ctx": sibling}, device_id_type=MESH,
        )

    def pre_twin():
        return pltpu.make_async_remote_copy(
            head(staged, chip), pre_all.at[:, :, me], pre_pass.at[0], pre_recv.at[me],
            device_id={"ctx": sibling}, device_id_type=MESH,
        )

    own = [
        pltpu.make_async_copy(
            q_ref.at[:, pl.ds(pl.multiple_of(me * width, width), width)],
            q_all.at[pl.ds(pl.multiple_of(me * rows, rows), rows), :],
            near.at[0],
        ),
        pltpu.make_async_copy(head(new_ref, chip), kv_slot(me), near.at[1]),
        pltpu.make_async_copy(head(staged, chip), pre_all.at[:, :, me], near.at[2]),
    ]

    def each(count, act, first=1):
        def step(t, c):
            act(t)
            return c

        lax.fori_loop(first, count, step, 0)

    each(groups, lambda t: page_copy(t).start())
    each(chips, lambda t: kv_copy(t).start())
    each(columns, lambda t: q_copy(t).start())
    kv_twin().start()
    own[0].start()
    own[1].start()

    def page_arrival(t):
        source = (group + groups - t) % groups
        pltpu.make_async_remote_copy(
            outgoing.at[source], arrived.at[source], req_send.at[0], req_recv.at[source],
            device_id={"req": source}, device_id_type=MESH,
        ).wait_recv()

    each(groups, page_arrival)
    for i in range(staged.shape[1]):
        page = arrived[jnp.maximum(owners[0, 0, i], 0)]
        staged[:, i] = page
    each(chips, lambda t: pre_copy(t).start())
    pre_twin().start()
    own[2].start()

    def kv_relay(t):
        kv_onward(t).wait_recv()
        kv_onward(t).start()

    def pre_relay(t):
        pre_onward(t).wait_recv()
        pre_onward(t).start()

    each(chips, kv_relay)
    each(chips, pre_relay)

    def q_arrival(t):
        source = (me + columns - t) % columns
        pltpu.make_async_remote_copy(
            q_all.at[pl.ds(pl.multiple_of(source * rows, rows), rows), :],
            q_all.at[pl.ds(pl.multiple_of(source * rows, rows), rows), :],
            q_send.at[0], q_recv.at[source], device_id={"ctx": source}, device_id_type=MESH,
        ).wait_recv()

    each(columns, q_arrival)

    def twin_arrival(t):
        source = ((chip + t) % chips) * 2 + (1 - core)
        for slot, sem in ((kv_slot(source), kv_recv), (pre_all.at[:, :, source], pre_recv)):
            pltpu.make_async_remote_copy(
                slot, slot, near.at[3], sem.at[source],
                device_id={"ctx": sibling}, device_id_type=MESH,
            ).wait_recv()

    each(chips, twin_arrival, 0)
    each(groups, lambda t: page_copy(t).wait_send())
    each(columns, lambda t: q_copy(t).wait_send())
    each(chips, lambda t: kv_copy(t).wait_send())
    each(chips, lambda t: pre_copy(t).wait_send())
    each(chips, lambda t: kv_onward(t).wait_send())
    each(chips, lambda t: pre_onward(t).wait_send())
    kv_twin().wait_send()
    pre_twin().wait_send()
    for copy in own:
        copy.wait()


def gather(wanted, owners, pool, queries, kv_new, columns, groups):
    rows, features = queries.shape
    slots, page_len = owners.shape[2], pool.shape[2]
    dtype = queries.dtype
    dma = pltpu.SemaphoreType.DMA
    anywhere = pl.BlockSpec(memory_space=pl.ANY)
    chips = columns // 2
    return pl.pallas_call(
        lambda *refs: gather_kernel(columns, groups, *refs),
        out_shape=(
            jax.ShapeDtypeStruct((rows * columns, features // columns), dtype),
            jax.ShapeDtypeStruct((2, rows * columns, HEAD), dtype),
            jax.ShapeDtypeStruct((2, slots, columns, page_len, HEAD), dtype),
        ),
        in_specs=[
            pl.BlockSpec(memory_space=pltpu.SMEM),
            pl.BlockSpec(memory_space=pltpu.SMEM),
            pl.BlockSpec(memory_space=pltpu.VMEM),
            anywhere,
            anywhere,
        ],
        out_specs=(anywhere, anywhere, anywhere),
        scratch_shapes=[
            pltpu.VMEM((groups,) + pool.shape[1:], dtype),
            pltpu.VMEM((groups,) + pool.shape[1:], dtype),
            pltpu.VMEM((2, slots) + pool.shape[2:], dtype),
            dma((groups,)), dma((groups,)),
            dma((columns,)), dma((columns,)),
            dma((chips,)), dma((columns,)), dma((chips,)),
            dma((chips,)), dma((columns,)), dma((chips,)),
            dma((4,)),
        ],
        compiler_params=pltpu.CompilerParams(
            collective_id=0, has_side_effects=True, vmem_limit_bytes=16 << 20
        ),
        name="gather",
    )(wanted, owners, pool, queries, kv_new)


def new_kernel(info, q_ref, kv_ref, acc_ref, stat_ref):
    block = pl.program_id(0)
    rows, width = q_ref.shape
    heads = width // HEAD
    per = rows // TILE
    row = lax.broadcasted_iota(jnp.int32, (rows, 1), 0)
    low = jnp.full((rows, 1), info[block * per] * TILE, jnp.int32)
    for t in range(1, per):
        low = jnp.where(row >= t * TILE, info[block * per + t] * TILE, low)
    position = row + block * rows
    queries = [q_ref[:, h * HEAD : (h + 1) * HEAD] for h in range(heads)]

    def visible(at, size, last):
        column = lax.broadcasted_iota(jnp.int32, (rows, size), 1) + at
        seen = column >= low
        return seen & (column <= position) if last else seen

    def fold(at, size, states):
        keys, values = kv_ref[0, pl.ds(at, size), :], kv_ref[1, pl.ds(at, size), :]
        seen = visible(at, size, states is None)
        result = []
        for h in range(heads):
            scores = jnp.where(seen, scores_of(queries[h], keys), FILL)
            top = jnp.max(scores, axis=1, keepdims=True)
            if states is not None:
                top = jnp.maximum(top, states[h][0])
            weights = decay(scores, top)
            total = jnp.sum(weights, axis=1, keepdims=True)
            acc = jnp.dot(
                weights.astype(jnp.bfloat16), values, preferred_element_type=jnp.float32
            )
            if states is not None:
                shrink = decay(states[h][0], top)
                total = total + states[h][1] * shrink
                acc = acc + states[h][2] * shrink
            result.append((top, total, acc))
        return tuple(result)

    def whole(index):
        return pl.multiple_of(index * rows, rows)

    begin = info[block * per] // per
    count = block - begin
    states = fold(whole(block), rows, None)
    states = lax.fori_loop(
        0, count // 4, lambda i, s: fold(whole(begin + i * 4), 4 * rows, s), states
    )
    states = lax.cond(
        count % 4 >= 2, lambda s: fold(whole(block - count % 4), 2 * rows, s), lambda s: s, states
    )
    states = lax.cond(count % 2 == 1, lambda s: fold(whole(block - 1), rows, s), lambda s: s, states)
    lane = lax.broadcasted_iota(jnp.int32, stat_ref.shape, 1)
    stat = jnp.zeros(stat_ref.shape, jnp.float32)
    for h in range(heads):
        acc_ref[:, h * HEAD : (h + 1) * HEAD] = states[h][2]
        stat = jnp.where(lane == 2 * h, states[h][0], stat)
        stat = jnp.where(lane == 2 * h + 1, states[h][1], stat)
    stat_ref[...] = stat


def attend_new(starts, queries, kv, rows):
    positions, width = queries.shape
    return pl.pallas_call(
        new_kernel,
        out_shape=(
            jax.ShapeDtypeStruct((positions, width), jnp.float32),
            jax.ShapeDtypeStruct((positions, HEAD), jnp.float32),
        ),
        grid_spec=pltpu.PrefetchScalarGridSpec(
            num_scalar_prefetch=1,
            grid=(positions // rows,),
            in_specs=[
                pl.BlockSpec((rows, width), lambda i, s: (i, 0)),
                pl.BlockSpec(kv.shape, lambda i, s: (0, 0, 0)),
            ],
            out_specs=(
                pl.BlockSpec((rows, width), lambda i, s: (i, 0)),
                pl.BlockSpec((rows, HEAD), lambda i, s: (i, 0)),
            ),
        ),
        compiler_params=pltpu.CompilerParams(
            dimension_semantics=("arbitrary",), vmem_limit_bytes=32 << 20
        ),
        name="attend_new",
    )(starts, queries, kv)


def finish_kernel(
    columns, pages, q_ref, pre_ref, acc_ref, stat_ref, out_ref, stage, send, recv, near
):
    me = lax.axis_index("ctx")
    positions, width = q_ref.shape
    rows = positions // columns
    heads = width // HEAD
    keys = pre_ref.shape[1]

    barrier = pltpu.get_barrier_semaphore()

    def greet(t, c):
        pl.semaphore_signal(
            barrier, inc=1, device_id={"ctx": (me + t) % columns}, device_id_type=MESH
        )
        return c

    lax.fori_loop(1, columns, greet, 0)
    pl.semaphore_wait(barrier, columns - 1)
    live = pages[0] * (keys // 64)

    def compute(block):
        at = pl.ds(pl.multiple_of(block * rows, rows), rows)
        for h in range(heads):
            cut = slice(h * HEAD, (h + 1) * HEAD)
            scores = scores_of(q_ref[at, cut], pre_ref[0])
            half = keys // 2
            column = lax.broadcasted_iota(jnp.int32, (rows, half), 1) + half
            scores = jnp.concatenate(
                [scores[:, :half], jnp.where(column < live, scores[:, half:], FILL)], axis=1
            )
            before = stat_ref[at, 2 * h : 2 * h + 1]
            top = jnp.maximum(jnp.max(scores, axis=1, keepdims=True), before)
            weights = decay(scores, top)
            shrink = decay(before, top)
            total = jnp.sum(weights, axis=1, keepdims=True)
            total = total + stat_ref[at, 2 * h + 1 : 2 * h + 2] * shrink
            acc = jnp.dot(
                weights.astype(jnp.bfloat16), pre_ref[1], preferred_element_type=jnp.float32
            )
            acc = acc + acc_ref[at, cut] * shrink
            stage[at, cut] = (acc / total).astype(stage.dtype)

    def cut_of(device):
        return out_ref.at[:, pl.ds(pl.multiple_of(device * width, width), width)]

    def staged(block):
        return stage.at[pl.ds(pl.multiple_of(block * rows, rows), rows), :]

    def out_copy(t):
        to = (me + t) % columns
        return pltpu.make_async_remote_copy(
            staged(to), cut_of(me), send.at[t], recv.at[me],
            device_id={"ctx": to}, device_id_type=MESH,
        )

    def step(i, c):
        t = columns - 1 - i
        compute((me + t) % columns)
        out_copy(t).start()
        return c

    lax.fori_loop(0, columns - 1, step, 0)
    compute(me)
    mine = pltpu.make_async_copy(staged(me), cut_of(me), near)
    mine.start()

    def settle(t, c):
        source = (me + t) % columns
        pltpu.make_async_remote_copy(
            staged(source), cut_of(source), send.at[0], recv.at[source],
            device_id={"ctx": source}, device_id_type=MESH,
        ).wait_recv()
        out_copy(t).wait_send()
        return c

    lax.fori_loop(1, columns, settle, 0)
    mine.wait()


def finish(pages, queries, pre, acc, stat, columns):
    positions, width = queries.shape
    vmem = pl.BlockSpec(memory_space=pltpu.VMEM)
    return pl.pallas_call(
        lambda *refs: finish_kernel(columns, *refs),
        out_shape=jax.ShapeDtypeStruct((positions // columns, width * columns), queries.dtype),
        in_specs=[pl.BlockSpec(memory_space=pltpu.SMEM), vmem, vmem, vmem, vmem],
        out_specs=pl.BlockSpec(memory_space=pl.ANY),
        scratch_shapes=[
            pltpu.VMEM((positions, width), queries.dtype),
            pltpu.SemaphoreType.DMA((columns,)),
            pltpu.SemaphoreType.DMA((columns,)),
            pltpu.SemaphoreType.DMA,
        ],
        compiler_params=pltpu.CompilerParams(
            collective_id=1, has_side_effects=True, vmem_limit_bytes=40 << 20
        ),
        name="finish",
    )(pages, queries, pre, acc, stat)


def local(queries, kv_new, kv_pool, prefix_pages, reader_owner, send_page, tile_doc):
    columns, groups = lax.axis_size("ctx"), lax.axis_size("req")
    rows = queries.shape[1]
    q, kv, pre = gather(
        send_page, reader_owner, kv_pool, queries[0], kv_new[0], columns, groups
    )
    pre = pre.reshape(2, -1, HEAD)
    docs = tile_doc[0]
    starts = jnp.sum((docs[None, :] < docs[:, None]).astype(jnp.int32), axis=1)
    acc, stat = attend_new(starts, q, kv, rows)
    return finish(prefix_pages, q, pre, acc, stat, columns)[None]


def solution(mesh):
    in_specs = (
        P("req", "ctx", None),
        P("req", None, "ctx", None),
        P(("req", "ctx"), None, None, None),
        P("req"),
        P("req", "ctx", None),
        P("req", "ctx", None),
        P("req", None),
    )
    return jax.shard_map(
        local, mesh=mesh, in_specs=in_specs, out_specs=P("req", "ctx", None), check_vma=False
    )
```

time: 254 us -> 158 us (0.62)
  waiting for transfers between devices: 67.6 us -> 0 us
  Pallas kernels: 84.8 us -> 150 us
  blocking collectives: 33.1 us -> 0 us
  local copies, waits for them, and re-layouts: 32.1 us -> 6.5 us
  starting transfers between devices: 24.5 us -> 0 us
  between operations: 8.34 us -> 0.69 us
    all_to_all x3 -> x0, waiting for transfers between devices: 67.6 us -> none  [the longest x1 34.6 us: local(): kv = lax.all_to_all(block, 'ctx', split_axis=0, concat_axis=0, tiled=True)]
    pallas_call x1 -> x3, Pallas kernels: 84.8 us -> 150 us  [the longest x1 67.5 us: gather(): pl.pallas_call(lambda *refs: gather_kernel(columns, groups, *refs), out_s...]
    all_to_all x1 -> x0, blocking collectives: 33.1 us -> none  [local(): out = lax.all_to_all(out, 'ctx', split_axis=0, concat_axis=1, tiled=True)]
    all_to_all x3 -> x0, starting transfers between devices: 24.5 us -> none  [the longest x1 10.3 us: local(): lax.all_to_all(queries[0], 'ctx', split_axis=1, concat_axis=0, tiled=True)]
    unnamed x18 -> x13, local copies, waits for them, and re-layouts: 15.3 us -> 6.5 us
    broadcast_in_dim x2 -> x0, local copies, waits for them, and re-layouts: 4.88 us -> none  [the longest x1 2.54 us: local(): block = jnp.repeat(jnp.transpose(block, (2, 0, 1, 3)), copies, axis=0)]
    transpose x5 -> x0, local copies, waits for them, and re-layouts: 3.66 us -> none  [the longest x2 3.25 us: local(): new_kv = jnp.transpose(kv[:, :, :rows], (1, 0, 2, 3)).reshape(2, -1, HEAD)]
    slice x4 -> x0, local copies, waits for them, and re-layouts: 3.48 us -> none  [the longest x2 2.25 us: pick(): ids[i]]
  transfers between devices with their start and end apart: 3 -> 0, of which waited for: 3 -> 0; matrix products, arithmetic and copies ran while one was open for 3% -> 0% of each run, Pallas kernels for 0% -> 0%
where the time goes in v2:
time: 158 us; the launch traced here: 157 us
  Pallas kernels  150 us (95%)
  local copies, waits for them, and re-layouts  6.5 us (4%)
    pallas_call x1, Pallas kernels, gather(): pl.pallas_call(lambda *refs: gather_kernel(columns, groups, *refs), out_s...  67.5 us
    pallas_call x1, Pallas kernels, finish(): pl.pallas_call(lambda *refs: finish_kernel(columns, *refs), out_shape=jax...  47.4 us
    pallas_call x1, Pallas kernels, attend_new(): pl.pallas_call(new_kernel, out_shape=(jax.ShapeDtypeStruct((positions, wi...  35.2 us
    unnamed x13, local copies, waits for them, and re-layouts  6.5 us

profile of v2, /device:TPU:10, one launch (start us, length us, event | category | flops | bytes accessed | tf_op | source)
XLA Modules:
  0.0 157.5 jit_solution(17092087581202913241)
XLA Ops:
  0.0 0.0 copy-start.5
  0.0 0.0 copy-start
  0.0 1.6 %copy-done = bf16[1,256,4096]{2,1,0:T(8,128)(2,1)S(1)} copy-done((bf16[1,256,4096]{2,1,0:T(8,128)(2,1)S(1)}, bf16[1,256,4096]{2,1,0:T(8,128)(2,1)}, u32[]{:S(2)}) %copy-start) | copy-done | bytes 2097176
  1.6 0.0 copy-start.1
  1.6 1.2 copy-done.1
  2.8 0.0 copy-start.2
  2.8 1.0 copy-done.2
  3.9 0.0 copy-start.3
  3.9 0.7 copy-done.3
  4.5 0.0 copy-start.4
  4.5 0.7 copy-done.4
  5.2 67.5 %gather.1 = (bf16[4096,256]{1,0:T(8,128)(2,1)S(1)}, bf16[2,4096,128]{2,1,0:T(8,128)(2,1)S(1)}, bf16[2,4,16,32,128]{4,3,2,1,0:T(8,128)(2,1)S(1)}) custom-call(s32[1,1,8]{2,1,0:T(1,128)S(1)} %copy-done.3, s32[1,1,4]{2,1,0:T(1,128)S(1)} %copy-done.4, bf16[4,2,32,1024]{3,2,1,0:T(8,128)(2,1)S(1)} %copy-done.2, bf16[256,4096]{1,0:T(8,128)(2,1)S(1)} %bitcast.6, ...), custom_call_target="tpu_custom_call" | custom-call | tf_op jit(solution)/shard_map/gather/pallas_call | solution.py:215
  72.7 0.0 copy-done.5
  72.7 0.2 convert_reduce_fusion.info
  72.9 35.2 %attend_new.1 = (f32[4096,256]{1,0:T(8,128)S(1)}, f32[4096,128]{1,0:T(8,128)S(1)}) custom-call(s32[32]{0:T(128)S(1)} %convert_reduce_fusion.info, bf16[4096,256]{1,0:T(8,128)(2,1)S(1)} %get-tuple-element.10.q_ref.refs_1_, bf16[2,4096,128]{2,1,0:T(8,128)(2,1)S(1)} %get-tuple-element.12.kv_ref), custom_call_target="tpu_custom_call" | custom-call | tf_op jit(solution)/shard_map/attend_new/pallas_call | solution.py:309
  108.8 47.4 %finish.1 = bf16[256,4096]{1,0:T(8,128)(2,1)S(1)} custom-call(s32[1]{0:T(128)S(6)} %copy.9.refs_0_, bf16[4096,256]{1,0:T(8,128)(2,1)S(1)} %get-tuple-element.10.q_ref.refs_1_, bf16[2,2048,128]{2,1,0:T(8,128)(2,1)S(1)} %bitcast.7, f32[4096,256]{1,0:T(8,128)S(1)} %get-tuple-element.13.refs_3_, f32[4096,128]{1,0:T(8,128)S(1)} %get-tuple-element.14.refs_4_), custom_call_target="tpu_custom_call" | custom-call | tf_op jit(solution)/shard_map/finish/pallas_call | solution.py:417
  156.1 1.3 copy.10
Async XLA Ops:
  0.0 72.7 %copy-start.5 = (s32[1,32]{1,0:T(1,128)S(1)}, s32[1,32]{1,0:T(1,128)}, u32[]{:S(2)}) copy-start(s32[1,32]{1,0:T(1,128)} %param.13) | copy-start | bytes 388
  0.0 1.6 %copy-start = (bf16[1,256,4096]{2,1,0:T(8,128)(2,1)S(1)}, bf16[1,256,4096]{2,1,0:T(8,128)(2,1)}, u32[]{:S(2)}) copy-start(bf16[1,256,4096]{2,1,0:T(8,128)(2,1)} %param.7) | copy-start | bytes 6291460
  1.6 1.2 copy-start.1
  2.8 1.0 copy-start.2
  3.9 0.7 copy-start.3
  4.5 0.7 copy-start.4

commit v3 on v0

v3 whole, which is shorter than its diff:
```python
import math

import jax
import jax.numpy as jnp
from jax import lax
from jax.experimental import pallas as pl
from jax.experimental.pallas import tpu as pltpu
from jax.sharding import PartitionSpec as P

HEAD = 128
TILE = 128
FILL = -1e30
SCALE = math.log2(math.e) / math.sqrt(HEAD)
MESH = pl.DeviceIdType.MESH
EARLY = 10
FIRST = 4


def scores_of(queries, keys):
    return lax.dot_general(
        queries, keys, (((1,), (1,)), ((), ())), preferred_element_type=jnp.float32
    )


def decay(scores, top):
    return jnp.exp2((scores - top) * SCALE)


def prefix_part(queries, pre_ref, live):
    keys = pre_ref.shape[1]
    half = keys // 2
    scores = scores_of(queries, pre_ref[0])
    column = lax.broadcasted_iota(jnp.int32, (queries.shape[0], half), 1) + half
    scores = jnp.concatenate(
        [scores[:, :half], jnp.where(column < live, scores[:, half:], FILL)], axis=1
    )
    top = jnp.max(scores, axis=1, keepdims=True)
    weights = decay(scores, top)
    total = jnp.sum(weights, axis=1, keepdims=True)
    acc = jnp.dot(weights.astype(jnp.bfloat16), pre_ref[1], preferred_element_type=jnp.float32)
    return top, total, acc


def joined(one, two):
    top = jnp.maximum(one[0], two[0])
    left, right = decay(one[0], top), decay(two[0], top)
    return top, one[1] * left + two[1] * right, one[2] * left + two[2] * right


def pack(tops_and_totals):
    shape = (tops_and_totals[0].shape[0], HEAD)
    lane = lax.broadcasted_iota(jnp.int32, shape, 1)
    stat = jnp.zeros(shape, jnp.float32)
    for at, column in enumerate(tops_and_totals):
        stat = jnp.where(lane == at, column, stat)
    return stat


def part_of(acc_ref, stat_ref, at, h):
    return (
        stat_ref[at, 2 * h : 2 * h + 1],
        stat_ref[at, 2 * h + 1 : 2 * h + 2],
        acc_ref[at, h * HEAD : (h + 1) * HEAD],
    )


def span(index, size):
    start = index * size
    return pl.ds(start if isinstance(start, int) else pl.multiple_of(start, size), size)


def partner(me, r, columns, sends):
    chips_x = columns // 4
    x, z, core = me // 4, (me // 2) % 2, me % 2
    x = (x + r // 4) % chips_x if sends else (x + chips_x - r // 4) % chips_x
    return x * 4 + ((z + r) % 2) * 2 + (core + r // 2) % 2


def partner_chip(chip, t, chips, sends):
    chips_x = chips // 2
    x, z = chip // 2, chip % 2
    x = (x + t // 2) % chips_x if sends else (x + chips_x - t // 2) % chips_x
    return x * 2 + (z + t) % 2


def each(first, last, act):
    def step(t, c):
        act(t)
        return c

    lax.fori_loop(first, last, step, 0)


def gather_kernel(
    columns, groups, early, wanted, owners, pages, pool_ref, q_ref, new_ref,
    q_all, kv_all, pre_all, acc_ref, stat_ref,
    pool, outgoing, arrived, staged, req_send, req_recv, q_send, q_recv, kv_send, kv_recv,
    kv_pass, pre_send, pre_recv, pre_pass, near,
):
    me = lax.axis_index("ctx")
    group = lax.axis_index("req")
    chips = columns // 2
    chip = me // 2
    core = me % 2
    sibling = chip * 2 + (1 - core)
    rows = q_ref.shape[0]
    width = q_all.shape[1]
    heads = width // HEAD
    slots, page_len = staged.shape[1], staged.shape[2]
    first = FIRST
    pool_copy = pltpu.make_async_copy(pool_ref, pool, near.at[3])
    pool_copy.start()

    barrier = pltpu.get_barrier_semaphore()

    def greet_column(r):
        to = partner(me, r, columns, True)
        pl.semaphore_signal(barrier, inc=1, device_id={"ctx": to}, device_id_type=MESH)

    def greet_group(t):
        to = (group + t) % groups
        pl.semaphore_signal(barrier, inc=1, device_id={"req": to}, device_id_type=MESH)

    each(1, groups, greet_group)
    each(1, columns, greet_column)
    pool_copy.wait()
    for g in range(groups):
        outgoing[g] = pool[jnp.maximum(wanted[0, 0, g], 0)]
    arrived[group] = outgoing[group]
    pl.semaphore_wait(barrier, columns + groups - 2)

    def page_copy(t):
        to = (group + t) % groups
        return pltpu.make_async_remote_copy(
            outgoing.at[to], arrived.at[group], req_send.at[t], req_recv.at[group],
            device_id={"req": to}, device_id_type=MESH,
        )

    def q_cut(device):
        return q_ref.at[:, span(device, width)]

    def q_slot(device):
        return q_all.at[span(device, rows), :]

    def kv_slot(device):
        return kv_all.at[:, span(device, rows), :]

    def pre_slot(device):
        return pre_all.at[:, :, device]

    def new_cut(at):
        return new_ref.at[:, :, span(at, HEAD)]

    def pre_cut(at):
        return staged.at[:, :, :, span(at, HEAD)]

    def q_copy(r):
        to = partner(me, r, columns, True)
        return pltpu.make_async_remote_copy(
            q_cut(to), q_slot(me), q_send.at[r], q_recv.at[me],
            device_id={"ctx": to}, device_id_type=MESH,
        )

    def kv_copy(t):
        to = partner_chip(chip, t, chips, True)
        return pltpu.make_async_remote_copy(
            new_cut(to), kv_slot(me), kv_send.at[t], kv_recv.at[me],
            device_id={"ctx": to * 2 + core}, device_id_type=MESH,
        )

    def pre_copy(t):
        to = partner_chip(chip, t, chips, True)
        return pltpu.make_async_remote_copy(
            pre_cut(to), pre_slot(me), pre_send.at[t], pre_recv.at[me],
            device_id={"ctx": to * 2 + core}, device_id_type=MESH,
        )

    def source_of(t):
        return partner_chip(chip, t, chips, False) * 2 + core

    def to_sibling(source_ref, slot, send, recv):
        return pltpu.make_async_remote_copy(
            source_ref, slot, send, recv, device_id={"ctx": sibling}, device_id_type=MESH
        )

    def kv_onward(t):
        slot = kv_slot(source_of(t))
        return to_sibling(slot, slot, kv_pass.at[t], kv_recv.at[source_of(t)])

    def pre_onward(t):
        slot = pre_slot(source_of(t))
        return to_sibling(slot, slot, pre_pass.at[t], pre_recv.at[source_of(t)])

    kv_twin = to_sibling(new_cut(chip), kv_slot(me), kv_pass.at[0], kv_recv.at[me])
    pre_twin = to_sibling(pre_cut(chip), pre_slot(me), pre_pass.at[0], pre_recv.at[me])
    own = [
        pltpu.make_async_copy(q_cut(me), q_slot(me), near.at[0]),
        pltpu.make_async_copy(new_cut(chip), kv_slot(me), near.at[1]),
        pltpu.make_async_copy(pre_cut(chip), pre_slot(me), near.at[2]),
    ]

    each(1, groups, lambda t: page_copy(t).start())
    each(1, first, lambda r: q_copy(r).start())
    own[0].start()
    own[1].start()

    def page_arrival(t):
        source = (group + groups - t) % groups
        pltpu.make_async_remote_copy(
            outgoing.at[source], arrived.at[source], req_send.at[0], req_recv.at[source],
            device_id={"req": source}, device_id_type=MESH,
        ).wait_recv()

    each(1, groups, page_arrival)
    for i in range(slots):
        staged[:, i] = arrived[jnp.maximum(owners[0, 0, i], 0)]
    each(1, chips, lambda t: pre_copy(t).start())
    pre_twin.start()
    own[2].start()
    each(first, columns, lambda r: q_copy(r).start())
    each(1, chips, lambda t: kv_copy(t).start())
    kv_twin.start()

    def pre_relay(t):
        pre_onward(t).wait_recv()
        pre_onward(t).start()

    each(1, chips, pre_relay)

    def pre_twin_arrival(t):
        source = partner_chip(chip, t, chips, False) * 2 + (1 - core)
        to_sibling(pre_slot(source), pre_slot(source), near.at[3], pre_recv.at[source]).wait_recv()

    each(0, chips, pre_twin_arrival)
    own[0].wait()
    own[2].wait()
    keys = slots * columns * page_len
    live = pages[0] * page_len
    prefix = pre_all.reshape(2, keys, HEAD)

    def q_arrival(r):
        source = partner(me, r, columns, False)
        pltpu.make_async_remote_copy(
            q_slot(source), q_slot(source), q_send.at[0], q_recv.at[source],
            device_id={"ctx": source}, device_id_type=MESH,
        ).wait_recv()

    def attend(r):
        at = span(partner(me, r, columns, False), rows)
        out = span(r, rows)
        found = []
        for h in range(heads):
            cut = slice(h * HEAD, (h + 1) * HEAD)
            top, total, acc = prefix_part(q_all[at, cut], prefix, live)
            acc_ref[out, cut] = acc
            found += [top, total]
        stat_ref[out, :] = pack(found)

    attend(0)

    def arrive_and_attend(r):
        q_arrival(r)
        attend(r)

    each(1, early, arrive_and_attend)

    def kv_relay(t):
        kv_onward(t).wait_recv()
        kv_onward(t).start()

    each(1, chips, kv_relay)
    each(early, columns, q_arrival)

    def kv_twin_arrival(t):
        source = partner_chip(chip, t, chips, False) * 2 + (1 - core)
        to_sibling(kv_slot(source), kv_slot(source), near.at[3], kv_recv.at[source]).wait_recv()

    each(0, chips, kv_twin_arrival)
    each(1, groups, lambda t: page_copy(t).wait_send())
    each(1, columns, lambda r: q_copy(r).wait_send())
    for copies in (kv_copy, pre_copy, kv_onward, pre_onward):
        each(1, chips, lambda t, copies=copies: copies(t).wait_send())
    kv_twin.wait_send()
    pre_twin.wait_send()
    own[1].wait()


def gather(wanted, owners, pages, pool, queries, kv_new, columns, groups, early):
    rows, features = queries.shape
    slots, page_len = owners.shape[2], pool.shape[2]
    dtype = queries.dtype
    width = features // columns
    dma = pltpu.SemaphoreType.DMA
    smem = pl.BlockSpec(memory_space=pltpu.SMEM)
    vmem = pl.BlockSpec(memory_space=pltpu.VMEM)
    hbm = pl.BlockSpec(memory_space=pltpu.HBM)
    chips = columns // 2
    return pl.pallas_call(
        lambda *refs: gather_kernel(columns, groups, early, *refs),
        out_shape=(
            jax.ShapeDtypeStruct((rows * columns, width), dtype),
            jax.ShapeDtypeStruct((2, rows * columns, HEAD), dtype),
            jax.ShapeDtypeStruct((2, slots, columns, page_len, HEAD), dtype),
            jax.ShapeDtypeStruct((rows * early, width), jnp.float32),
            jax.ShapeDtypeStruct((rows * early, HEAD), jnp.float32),
        ),
        in_specs=[smem, smem, smem, hbm, hbm, hbm],
        out_specs=(vmem, vmem, vmem, vmem, vmem),
        scratch_shapes=[
            pltpu.VMEM(pool.shape, dtype),
            pltpu.VMEM((groups,) + pool.shape[1:], dtype),
            pltpu.VMEM((groups,) + pool.shape[1:], dtype),
            pltpu.VMEM((2, slots) + pool.shape[2:], dtype),
            dma((groups,)), dma((groups,)),
            dma((columns,)), dma((columns,)),
            dma((chips,)), dma((columns,)), dma((chips,)),
            dma((chips,)), dma((columns,)), dma((chips,)),
            dma((4,)),
        ],
        compiler_params=pltpu.CompilerParams(
            collective_id=0, has_side_effects=True, vmem_limit_bytes=32 << 20
        ),
        name="gather",
    )(wanted, owners, pages, pool, queries, kv_new)


def new_kernel(
    early, docs, q_ref, kv_ref, acc_pre, stat_pre, done_ref, acc_ref, stat_ref, acc_s, stat_s, starts
):
    me = lax.axis_index("ctx")
    rows, width = acc_s.shape
    heads = width // HEAD
    per = rows // TILE
    positions = q_ref.shape[0]
    columns = positions // rows
    longest = 16 // per
    starts[0] = 0

    def begin_of(t):
        starts[t] = jnp.where(docs[0, t] == docs[0, t - 1], starts[t - 1], t)

    each(1, columns * per, begin_of)

    def do(slot, c):
        block = partner(me, slot, columns, False)
        begin = starts[block * per] // per
        count = block - begin
        row = lax.broadcasted_iota(jnp.int32, (rows, 1), 0)
        low = jnp.full((rows, 1), starts[block * per] * TILE, jnp.int32)
        for t in range(1, per):
            low = jnp.where(row >= t * TILE, starts[block * per + t] * TILE, low)
        low = low - begin * rows
        at = span(block, rows)

        def fold(before):
            size = (before + 1) * rows
            window = pl.ds(pl.multiple_of(begin * rows, rows), size)
            keys, values = kv_ref[0, window, :], kv_ref[1, window, :]
            column = lax.broadcasted_iota(jnp.int32, (rows, size), 1)
            seen = column >= low
            last = lax.broadcasted_iota(jnp.int32, (rows, rows), 1) <= row
            found = []
            for h in range(heads):
                cut = slice(h * HEAD, (h + 1) * HEAD)
                scores = scores_of(q_ref[at, cut], keys)
                tail = jnp.where(last, scores[:, before * rows :], FILL)
                if before:
                    tail = jnp.concatenate([scores[:, : before * rows], tail], axis=1)
                scores = jnp.where(seen, tail, FILL)
                top = jnp.max(scores, axis=1, keepdims=True)
                weights = decay(scores, top)
                found += [top, jnp.sum(weights, axis=1, keepdims=True)]
                acc_s[:, cut] = jnp.dot(
                    weights.astype(jnp.bfloat16), values, preferred_element_type=jnp.float32
                )
            stat_s[...] = pack(found)

        for before in range(longest + 1):
            pl.when(count == before)(lambda before=before: fold(before))

        @pl.when(slot < early)
        def _():
            here = span(slot, rows)
            for h in range(heads):
                _, total, acc = joined(
                    part_of(acc_s, stat_s, slice(None), h), part_of(acc_pre, stat_pre, here, h)
                )
                done_ref[here, h * HEAD : (h + 1) * HEAD] = (acc / total).astype(done_ref.dtype)

        @pl.when(slot >= early)
        def _():
            here = span(slot - early, rows)
            acc_ref[here, :] = acc_s[...]
            stat_ref[here, :] = stat_s[...]

        return c

    lax.fori_loop(0, positions // rows, do, 0)


def attend_new(docs, queries, kv, acc, stat, rows):
    positions, width = queries.shape
    early = acc.shape[0] // rows
    late = positions - rows * early
    smem = pl.BlockSpec(memory_space=pltpu.SMEM)
    vmem = pl.BlockSpec(memory_space=pltpu.VMEM)
    return pl.pallas_call(
        lambda *refs: new_kernel(early, *refs),
        out_shape=(
            jax.ShapeDtypeStruct((rows * early, width), queries.dtype),
            jax.ShapeDtypeStruct((late, width), jnp.float32),
            jax.ShapeDtypeStruct((late, HEAD), jnp.float32),
        ),
        in_specs=[smem, vmem, vmem, vmem, vmem],
        out_specs=(vmem, vmem, vmem),
        scratch_shapes=[
            pltpu.VMEM((rows, width), jnp.float32),
            pltpu.VMEM((rows, HEAD), jnp.float32),
            pltpu.SMEM((docs.shape[1],), jnp.int32),
        ],
        compiler_params=pltpu.CompilerParams(vmem_limit_bytes=40 << 20),
        name="attend_new",
    )(docs, queries, kv, acc, stat)


def finish_kernel(
    columns, early, pages, q_ref, pre_ref, done_ref, acc_ref, stat_ref, out_ref, stage, send, recv, near
):
    me = lax.axis_index("ctx")
    positions, width = q_ref.shape
    rows = positions // columns
    heads = width // HEAD
    live = pages[0] * (pre_ref.shape[1] // 64)

    barrier = pltpu.get_barrier_semaphore()

    def greet(r):
        to = partner(me, r, columns, False)
        pl.semaphore_signal(barrier, inc=1, device_id={"ctx": to}, device_id_type=MESH)

    each(1, columns, greet)
    pl.semaphore_wait(barrier, columns - 1)

    def cut_of(device):
        return out_ref.at[:, span(device, width)]

    def send_block(source, r):
        to = partner(me, r, columns, False)
        return pltpu.make_async_remote_copy(
            source, cut_of(me), send.at[r], recv.at[me], device_id={"ctx": to}, device_id_type=MESH
        )

    def send_early(r):
        send_block(done_ref.at[span(r, rows), :], r).start()

    each(1, early, send_early)
    mine = pltpu.make_async_copy(done_ref.at[0:rows, :], cut_of(me), near)
    mine.start()

    def late(i):
        at = span(partner(me, early + i, columns, False), rows)
        here = span(i, rows)
        for h in range(heads):
            cut = slice(h * HEAD, (h + 1) * HEAD)
            _, total, acc = joined(
                part_of(acc_ref, stat_ref, here, h), prefix_part(q_ref[at, cut], pre_ref, live)
            )
            stage[here, cut] = (acc / total).astype(stage.dtype)
        send_block(stage.at[here, :], early + i).start()

    each(0, columns - early, late)

    def settle(r):
        source = partner(me, r, columns, True)
        pltpu.make_async_remote_copy(
            done_ref.at[0:rows, :], cut_of(source), send.at[0], recv.at[source],
            device_id={"ctx": source}, device_id_type=MESH,
        ).wait_recv()
        send_block(done_ref.at[0:rows, :], r).wait_send()

    each(1, columns, settle)
    mine.wait()


def finish(pages, queries, pre, done, acc, stat, columns):
    positions, width = queries.shape
    rows = positions // columns
    early = done.shape[0] // rows
    vmem = pl.BlockSpec(memory_space=pltpu.VMEM)
    return pl.pallas_call(
        lambda *refs: finish_kernel(columns, early, *refs),
        out_shape=jax.ShapeDtypeStruct((rows, width * columns), queries.dtype),
        in_specs=[pl.BlockSpec(memory_space=pltpu.SMEM), vmem, vmem, vmem, vmem, vmem],
        out_specs=pl.BlockSpec(memory_space=pl.ANY),
        scratch_shapes=[
            pltpu.VMEM((positions - rows * early, width), queries.dtype),
            pltpu.SemaphoreType.DMA((columns,)),
            pltpu.SemaphoreType.DMA((columns,)),
            pltpu.SemaphoreType.DMA,
        ],
        compiler_params=pltpu.CompilerParams(
            collective_id=1, has_side_effects=True, vmem_limit_bytes=40 << 20
        ),
        name="finish",
    )(pages, queries, pre, done, acc, stat)


def local(queries, kv_new, kv_pool, prefix_pages, reader_owner, send_page, tile_doc):
    columns, groups = lax.axis_size("ctx"), lax.axis_size("req")
    rows = queries.shape[1]
    q, kv, pre, acc, stat = gather(
        send_page, reader_owner, prefix_pages, kv_pool, queries[0], kv_new[0], columns, groups, EARLY
    )
    done, acc, stat = attend_new(tile_doc, q, kv, acc, stat, rows)
    pre = pre.reshape(2, -1, HEAD)
    return finish(prefix_pages, q, pre, done, acc, stat, columns)[None]


def solution(mesh):
    in_specs = (
        P("req", "ctx", None),
        P("req", None, "ctx", None),
        P(("req", "ctx"), None, None, None),
        P("req"),
        P("req", "ctx", None),
        P("req", "ctx", None),
        P("req", None),
    )
    return jax.shard_map(
        local, mesh=mesh, in_specs=in_specs, out_specs=P("req", "ctx", None), check_vma=False
    )
```

time: 613 us -> 138 us (0.23)
  the two profiles are of different devices: /device:TPU:0 before, /device:TPU:10 now
where the time goes in v3:
time: 138 us; the launch traced here: 137 us
  Pallas kernels  130 us (94%)
  local copies, waits for them, and re-layouts  6.48 us (5%)
    pallas_call x1, Pallas kernels, gather(): pl.pallas_call(lambda *refs: gather_kernel(columns, groups, early, *refs)...  70 us
    pallas_call x1, Pallas kernels, finish(): pl.pallas_call(lambda *refs: finish_kernel(columns, early, *refs), out_sh...  34.5 us
    pallas_call x1, Pallas kernels, attend_new(): pl.pallas_call(lambda *refs: new_kernel(early, *refs), out_shape=(jax.Sha...  25.1 us
    unnamed x13, local copies, waits for them, and re-layouts  6.48 us

profile of v3, /device:TPU:10, one launch (start us, length us, event | category | flops | bytes accessed | tf_op | source)
XLA Modules:
  0.0 136.9 jit_solution(2449030503701710108)
XLA Ops:
  0.0 0.0 copy-start.5
  0.7 0.0 copy-start
  0.7 1.6 %copy-done = bf16[1,256,4096]{2,1,0:T(8,128)(2,1)S(1)} copy-done((bf16[1,256,4096]{2,1,0:T(8,128)(2,1)S(1)}, bf16[1,256,4096]{2,1,0:T(8,128)(2,1)}, u32[]{:S(2)}) %copy-start) | copy-done | bytes 2097176
  2.3 0.0 copy-start.1
  2.3 1.2 copy-done.1
  3.5 0.0 copy-start.2
  3.5 1.0 copy-done.2
  4.5 0.0 copy-start.3
  4.5 0.7 copy-done.3
  5.2 0.0 copy-start.4
  5.2 0.7 copy-done.4
  5.8 70.0 %gather.1 = (bf16[4096,256]{1,0:T(8,128)(2,1)S(1)}, bf16[2,4096,128]{2,1,0:T(8,128)(2,1)S(1)}, bf16[2,4,16,32,128]{4,3,2,1,0:T(8,128)(2,1)S(1)}, f32[2560,256]{1,0:T(8,128)S(1)}, f32[2560,128]{1,0:T(8,128)S(1)}) custom-call(s32[1,1,8]{2,1,0:T(1,128)S(1)} %copy-done.3, s32[1,1,4]{2,1,0:T(1,128)S(1)} %copy-done.4, s32[1]{0:T(128)S(6)} %copy.9.refs_2_.refs_0_, ...), custom_call_target="tpu_custom_call" | custom-call | tf_op jit(solution)/shard_map/gather/pallas_call | solution.py:298
  75.9 0.0 copy-done.5
  75.9 25.1 %attend_new.1 = (bf16[2560,256]{1,0:T(8,128)(2,1)S(1)}, f32[1536,256]{1,0:T(8,128)S(1)}, f32[1536,128]{1,0:T(8,128)S(1)}) custom-call(s32[1,32]{1,0:T(1,128)S(1)} %copy-done.5, bf16[4096,256]{1,0:T(8,128)(2,1)S(1)} %get-tuple-element.13.refs_1_, bf16[2,4096,128]{2,1,0:T(8,128)(2,1)S(1)} %get-tuple-element.15.refs_2_, ...), custom_call_target="tpu_custom_call" | custom-call | tf_op jit(solution)/shard_map/attend_new/pallas_call | solution.py:407
  101.0 34.5 %finish.1 = bf16[256,4096]{1,0:T(8,128)(2,1)S(1)} custom-call(s32[1]{0:T(128)S(6)} %copy.9.refs_2_.refs_0_, bf16[4096,256]{1,0:T(8,128)(2,1)S(1)} %get-tuple-element.13.refs_1_, bf16[2,2048,128]{2,1,0:T(8,128)(2,1)S(1)} %bitcast.7, bf16[2560,256]{1,0:T(8,128)(2,1)S(1)} %get-tuple-element.18.refs_3_, f32[1536,256]{1,0:T(8,128)S(1)} %get-tuple-element.19.refs_4_, ...), custom_call_target="tpu_custom_call" | custom-call | tf_op jit(solution)/shard_map/finish/pallas_call | solution.py:490
  135.6 1.3 copy.10
Async XLA Ops:
  0.0 75.9 %copy-start.5 = (s32[1,32]{1,0:T(1,128)S(1)}, s32[1,32]{1,0:T(1,128)}, u32[]{:S(2)}) copy-start(s32[1,32]{1,0:T(1,128)} %refs_0_.4) | copy-start | bytes 388
  0.7 1.6 %copy-start = (bf16[1,256,4096]{2,1,0:T(8,128)(2,1)S(1)}, bf16[1,256,4096]{2,1,0:T(8,128)(2,1)}, u32[]{:S(2)}) copy-start(bf16[1,256,4096]{2,1,0:T(8,128)(2,1)} %param.7) | copy-start | bytes 6291460
  2.3 1.2 copy-start.1
  3.5 1.0 copy-start.2
  4.5 0.7 copy-start.3
  5.2 0.7 copy-start.4

commit v4 on v3

--- a/solution.py
+++ b/solution.py
@@ -1,3 +1,4 @@
+import functools
 import math
 
 import jax
@@ -9,10 +10,12 @@
 
 HEAD = 128
 TILE = 128
+LONGEST = 16
+CHUNK = 512
 FILL = -1e30
 SCALE = math.log2(math.e) / math.sqrt(HEAD)
 MESH = pl.DeviceIdType.MESH
-EARLY = 10
+EARLY = 11
 FIRST = 4
 
 
@@ -26,19 +29,76 @@
     return jnp.exp2((scores - top) * SCALE)
 
 
-def prefix_part(queries, pre_ref, live):
+def attention(units, chunks):
+    def score(unit, chunk):
+        scores = scores_of(unit(), chunk[0]())
+        return scores if chunk[2] is None else jnp.where(chunk[2](), scores, FILL)
+
+    found = []
+    ahead = [score(units[0], chunk) for chunk in chunks]
+    for at in range(len(units)):
+        scores, ahead = ahead, []
+        top = functools.reduce(
+            jnp.maximum, [jnp.max(s, axis=1, keepdims=True) for s in scores]
+        )
+        total = acc = 0.0
+        for s, chunk in zip(scores, chunks):
+            if at + 1 < len(units):
+                ahead.append(score(units[at + 1], chunk))
+            weights = decay(s, top)
+            total = total + jnp.sum(weights, axis=1, keepdims=True)
+            acc = acc + jnp.dot(
+                weights.astype(jnp.bfloat16), chunk[1](), preferred_element_type=jnp.float32
+            )
+        found.append((top, total, acc))
+    return found
+
+
+def units_of(q_ref, at, heads):
+    return [lambda h=h: q_ref[at, h * HEAD : (h + 1) * HEAD] for h in range(heads)]
+
+
+def cuts(size):
+    return [(start, min(CHUNK, size - start)) for start in range(0, size, CHUNK)]
+
+
+def prefix_chunks(pre_ref, rows, live):
     keys = pre_ref.shape[1]
-    half = keys // 2
-    scores = scores_of(queries, pre_ref[0])
-    column = lax.broadcasted_iota(jnp.int32, (queries.shape[0], half), 1) + half
-    scores = jnp.concatenate(
-        [scores[:, :half], jnp.where(column < live, scores[:, half:], FILL)], axis=1
-    )
-    top = jnp.max(scores, axis=1, keepdims=True)
-    weights = decay(scores, top)
-    total = jnp.sum(weights, axis=1, keepdims=True)
-    acc = jnp.dot(weights.astype(jnp.bfloat16), pre_ref[1], preferred_element_type=jnp.float32)
-    return top, total, acc
+
+    def chunk(start, size):
+        def seen():
+            return lax.broadcasted_iota(jnp.int32, (rows, size), 1) < live - start
+
+        return (
+            lambda: pre_ref[0, start : start + size, :],
+            lambda: pre_ref[1, start : start + size, :],
+            seen if start + size > keys // 2 else None,
+        )
+
+    return [chunk(*cut) for cut in cuts(keys)]
+
+
+def new_chunk(kv_ref, start, size, seen):
+    window = pl.ds(pl.multiple_of(start, HEAD), size)
+    return (lambda: kv_ref[0, window, :], lambda: kv_ref[1, window, :], seen)
+
+
+def document_starts(docs, starts):
+    starts[0] = 0
+
+    def begin_of(t):
+        starts[t] = jnp.where(docs[0, t] == docs[0, t - 1], starts[t - 1], t)
+
+    each(1, docs.shape[1], begin_of)
+
+
+def first_seen(starts, block, rows):
+    per = rows // TILE
+    row = lax.broadcasted_iota(jnp.int32, (rows, 1), 0)
+    low = jnp.full((rows, 1), starts[block * per] * TILE, jnp.int32)
+    for t in range(1, per):
+        low = jnp.where(row >= t * TILE, starts[block * per + t] * TILE, low)
+    return row, low
 
 
 def joined(one, two):
@@ -92,9 +152,9 @@
 
 
 def gather_kernel(
-    columns, groups, early, wanted, owners, pages, pool_ref, q_ref, new_ref,
+    columns, groups, early, wanted_ref, owners_ref, pages, pool_ref, q_ref, new_ref,
     q_all, kv_all, pre_all, acc_ref, stat_ref,
-    pool, outgoing, arrived, staged, req_send, req_recv, q_send, q_recv, kv_send, kv_recv,
+    wanted, owners, pool, outgoing, arrived, staged, req_send, req_recv, q_send, q_recv, kv_send, kv_recv,
     kv_pass, pre_send, pre_recv, pre_pass, near,
 ):
     me = lax.axis_index("ctx")
@@ -108,8 +168,14 @@
     heads = width // HEAD
     slots, page_len = staged.shape[1], staged.shape[2]
     first = FIRST
-    pool_copy = pltpu.make_async_copy(pool_ref, pool, near.at[3])
-    pool_copy.start()
+    loads = [
+        pltpu.make_async_copy(source, here, near.at[3 + i])
+        for i, (source, here) in enumerate(
+            ((pool_ref, pool), (wanted_ref, wanted), (owners_ref, owners))
+        )
+    ]
+    for load in loads:
+        load.start()
 
     barrier = pltpu.get_barrier_semaphore()
 
@@ -123,7 +189,8 @@
 
     each(1, groups, greet_group)
     each(1, columns, greet_column)
-    pool_copy.wait()
+    for load in loads:
+        load.wait()
     for g in range(groups):
         outgoing[g] = pool[jnp.maximum(wanted[0, 0, g], 0)]
     arrived[group] = outgoing[group]
@@ -248,13 +315,10 @@
     def attend(r):
         at = span(partner(me, r, columns, False), rows)
         out = span(r, rows)
-        found = []
-        for h in range(heads):
-            cut = slice(h * HEAD, (h + 1) * HEAD)
-            top, total, acc = prefix_part(q_all[at, cut], prefix, live)
-            acc_ref[out, cut] = acc
-            found += [top, total]
-        stat_ref[out, :] = pack(found)
+        parts = attention(units_of(q_all, at, heads), prefix_chunks(prefix, rows, live))
+        for h, part in enumerate(parts):
+            acc_ref[out, h * HEAD : (h + 1) * HEAD] = part[2]
+        stat_ref[out, :] = pack([column for part in parts for column in part[:2]])
 
     attend(0)
 
@@ -283,6 +347,10 @@
     kv_twin.wait_send()
     pre_twin.wait_send()
     own[1].wait()
+
+
+def in_hbm(x):
+    return pltpu.with_memory_space_constraint(x, pltpu.HBM)
 
 
 def gather(wanted, owners, pages, pool, queries, kv_new, columns, groups, early):
@@ -304,9 +372,11 @@
             jax.ShapeDtypeStruct((rows * early, width), jnp.float32),
             jax.ShapeDtypeStruct((rows * early, HEAD), jnp.float32),
         ),
-        in_specs=[smem, smem, smem, hbm, hbm, hbm],
+        in_specs=[hbm, hbm, smem, hbm, hbm, hbm],
         out_specs=(vmem, vmem, vmem, vmem, vmem),
         scratch_shapes=[
+            pltpu.SMEM(wanted.shape, jnp.int32),
+            pltpu.SMEM(owners.shape, jnp.int32),
             pltpu.VMEM(pool.shape, dtype),
             pltpu.VMEM((groups,) + pool.shape[1:], dtype),
             pltpu.VMEM((groups,) + pool.shape[1:], dtype),
@@ -315,104 +385,71 @@
             dma((columns,)), dma((columns,)),
             dma((chips,)), dma((columns,)), dma((chips,)),
             dma((chips,)), dma((columns,)), dma((chips,)),
-            dma((4,)),
+            dma((6,)),
         ],
         compiler_params=pltpu.CompilerParams(
             collective_id=0, has_side_effects=True, vmem_limit_bytes=32 << 20
         ),
         name="gather",
-    )(wanted, owners, pages, pool, queries, kv_new)
-
-
-def new_kernel(
-    early, docs, q_ref, kv_ref, acc_pre, stat_pre, done_ref, acc_ref, stat_ref, acc_s, stat_s, starts
-):
+    )(
+        in_hbm(wanted), in_hbm(owners), pages, in_hbm(pool), in_hbm(queries), in_hbm(kv_new)
+    )
+
+
+def new_kernel(columns, docs, q_ref, kv_ref, acc_pre, stat_pre, done_ref, acc_s, stat_s, starts):
     me = lax.axis_index("ctx")
     rows, width = acc_s.shape
     heads = width // HEAD
     per = rows // TILE
-    positions = q_ref.shape[0]
-    columns = positions // rows
-    longest = 16 // per
-    starts[0] = 0
-
-    def begin_of(t):
-        starts[t] = jnp.where(docs[0, t] == docs[0, t - 1], starts[t - 1], t)
-
-    each(1, columns * per, begin_of)
-
-    def do(slot, c):
+    document_starts(docs, starts)
+
+    def do(slot):
         block = partner(me, slot, columns, False)
         begin = starts[block * per] // per
-        count = block - begin
-        row = lax.broadcasted_iota(jnp.int32, (rows, 1), 0)
-        low = jnp.full((rows, 1), starts[block * per] * TILE, jnp.int32)
-        for t in range(1, per):
-            low = jnp.where(row >= t * TILE, starts[block * per + t] * TILE, low)
-        low = low - begin * rows
+        row, low = first_seen(starts, block, rows)
         at = span(block, rows)
 
         def fold(before):
-            size = (before + 1) * rows
-            window = pl.ds(pl.multiple_of(begin * rows, rows), size)
-            keys, values = kv_ref[0, window, :], kv_ref[1, window, :]
-            column = lax.broadcasted_iota(jnp.int32, (rows, size), 1)
-            seen = column >= low
-            last = lax.broadcasted_iota(jnp.int32, (rows, rows), 1) <= row
-            found = []
-            for h in range(heads):
-                cut = slice(h * HEAD, (h + 1) * HEAD)
-                scores = scores_of(q_ref[at, cut], keys)
-                tail = jnp.where(last, scores[:, before * rows :], FILL)
-                if before:
-                    tail = jnp.concatenate([scores[:, : before * rows], tail], axis=1)
-                scores = jnp.where(seen, tail, FILL)
-                top = jnp.max(scores, axis=1, keepdims=True)
-                weights = decay(scores, top)
-                found += [top, jnp.sum(weights, axis=1, keepdims=True)]
-                acc_s[:, cut] = jnp.dot(
-                    weights.astype(jnp.bfloat16), values, preferred_element_type=jnp.float32
-                )
-            stat_s[...] = pack(found)
-
-        for before in range(longest + 1):
-            pl.when(count == before)(lambda before=before: fold(before))
-
-        @pl.when(slot < early)
-        def _():
-            here = span(slot, rows)
-            for h in range(heads):
-                _, total, acc = joined(
-                    part_of(acc_s, stat_s, slice(None), h), part_of(acc_pre, stat_pre, here, h)
-                )
-                done_ref[here, h * HEAD : (h + 1) * HEAD] = (acc / total).astype(done_ref.dtype)
-
-        @pl.when(slot >= early)
-        def _():
-            here = span(slot - early, rows)
-            acc_ref[here, :] = acc_s[...]
-            stat_ref[here, :] = stat_s[...]
-
-        return c
-
-    lax.fori_loop(0, positions // rows, do, 0)
+            def seen(start, size):
+                return lax.broadcasted_iota(jnp.int32, (rows, size), 1) + start >= low
+
+            def chunk(offset, size):
+                start = begin * rows + offset
+                return new_chunk(kv_ref, start, size, lambda: seen(start, size))
+
+            def last():
+                column = lax.broadcasted_iota(jnp.int32, (rows, rows), 1)
+                return seen(block * rows, rows) & (column <= row)
+
+            chunks = [chunk(*cut) for cut in cuts(before * rows)]
+            chunks.append(new_chunk(kv_ref, block * rows, rows, last))
+            parts = attention(units_of(q_ref, at, heads), chunks)
+            for h, part in enumerate(parts):
+                acc_s[:, h * HEAD : (h + 1) * HEAD] = part[2]
+            stat_s[...] = pack([column for part in parts for column in part[:2]])
+
+        for before in range(LONGEST // per + 1):
+            pl.when(block - begin == before)(lambda before=before: fold(before))
+
+        here = span(slot, rows)
+        for h in range(heads):
+            _, total, acc = joined(
+                part_of(acc_s, stat_s, slice(None), h), part_of(acc_pre, stat_pre, here, h)
+            )
+            done_ref[here, h * HEAD : (h + 1) * HEAD] = (acc / total).astype(done_ref.dtype)
+
+    each(0, done_ref.shape[0] // rows, do)
 
 
 def attend_new(docs, queries, kv, acc, stat, rows):
     positions, width = queries.shape
-    early = acc.shape[0] // rows
-    late = positions - rows * early
     smem = pl.BlockSpec(memory_space=pltpu.SMEM)
     vmem = pl.BlockSpec(memory_space=pltpu.VMEM)
     return pl.pallas_call(
-        lambda *refs: new_kernel(early, *refs),
-        out_shape=(
-            jax.ShapeDtypeStruct((rows * early, width), queries.dtype),
-            jax.ShapeDtypeStruct((late, width), jnp.float32),
-            jax.ShapeDtypeStruct((late, HEAD), jnp.float32),
-        ),
+        lambda *refs: new_kernel(positions // rows, *refs),
+        out_shape=jax.ShapeDtypeStruct(acc.shape, queries.dtype),
         in_specs=[smem, vmem, vmem, vmem, vmem],
-        out_specs=(vmem, vmem, vmem),
+        out_specs=vmem,
         scratch_shapes=[
             pltpu.VMEM((rows, width), jnp.float32),
             pltpu.VMEM((rows, HEAD), jnp.float32),
@@ -424,12 +461,13 @@
 
 
 def finish_kernel(
-    columns, early, pages, q_ref, pre_ref, done_ref, acc_ref, stat_ref, out_ref, stage, send, recv, near
+    columns, pages, docs, q_ref, pre_ref, kv_ref, done_ref, out_ref, stage, starts, send, recv, near
 ):
     me = lax.axis_index("ctx")
     positions, width = q_ref.shape
     rows = positions // columns
     heads = width // HEAD
+    early = done_ref.shape[0] // rows
     live = pages[0] * (pre_ref.shape[1] // 64)
 
     barrier = pltpu.get_barrier_semaphore()
@@ -439,6 +477,7 @@
         pl.semaphore_signal(barrier, inc=1, device_id={"ctx": to}, device_id_type=MESH)
 
     each(1, columns, greet)
+    document_starts(docs, starts)
     pl.semaphore_wait(barrier, columns - 1)
 
     def cut_of(device):
@@ -450,22 +489,30 @@
             source, cut_of(me), send.at[r], recv.at[me], device_id={"ctx": to}, device_id_type=MESH
         )
 
-    def send_early(r):
-        send_block(done_ref.at[span(r, rows), :], r).start()
-
-    each(1, early, send_early)
+    each(1, early, lambda r: send_block(done_ref.at[span(r, rows), :], r).start())
     mine = pltpu.make_async_copy(done_ref.at[0:rows, :], cut_of(me), near)
     mine.start()
+    longest = LONGEST * TILE // rows
 
     def late(i):
-        at = span(partner(me, early + i, columns, False), rows)
+        block = partner(me, early + i, columns, False)
+        row, low = first_seen(starts, block, rows)
+        begin = jnp.maximum(block - longest, 0) * rows
+
+        def chunk(offset, size):
+            start = begin + offset
+
+            def seen():
+                column = lax.broadcasted_iota(jnp.int32, (rows, size), 1) + start
+                return (column >= low) & (column <= row + block * rows)
+
+            return new_chunk(kv_ref, start, size, seen)
+
+        chunks = prefix_chunks(pre_ref, rows, live)
+        chunks += [chunk(*cut) for cut in cuts((longest + 1) * rows)]
         here = span(i, rows)
-        for h in range(heads):
-            cut = slice(h * HEAD, (h + 1) * HEAD)
-            _, total, acc = joined(
-                part_of(acc_ref, stat_ref, here, h), prefix_part(q_ref[at, cut], pre_ref, live)
-            )
-            stage[here, cut] = (acc / total).astype(stage.dtype)
+        for h, part in enumerate(attention(units_of(q_ref, span(block, rows), heads), chunks)):
+            stage[here, h * HEAD : (h + 1) * HEAD] = (part[2] / part[1]).astype(stage.dtype)
         send_block(stage.at[here, :], early + i).start()
 
     each(0, columns - early, late)
@@ -482,18 +529,18 @@
     mine.wait()
 
 
-def finish(pages, queries, pre, done, acc, stat, columns):
+def finish(pages, docs, queries, pre, kv, done, columns):
     positions, width = queries.shape
-    rows = positions // columns
-    early = done.shape[0] // rows
+    smem = pl.BlockSpec(memory_space=pltpu.SMEM)
     vmem = pl.BlockSpec(memory_space=pltpu.VMEM)
     return pl.pallas_call(
-        lambda *refs: finish_kernel(columns, early, *refs),
-        out_shape=jax.ShapeDtypeStruct((rows, width * columns), queries.dtype),
-        in_specs=[pl.BlockSpec(memory_space=pltpu.SMEM), vmem, vmem, vmem, vmem, vmem],
+        lambda *refs: finish_kernel(columns, *refs),
+        out_shape=jax.ShapeDtypeStruct((positions // columns, width * columns), queries.dtype),
+        in_specs=[smem, smem, vmem, vmem, vmem, vmem],
         out_specs=pl.BlockSpec(memory_space=pl.ANY),
         scratch_shapes=[
-            pltpu.VMEM((positions - rows * early, width), queries.dtype),
+            pltpu.VMEM((positions - done.shape[0], width), queries.dtype),
+            pltpu.SMEM((docs.shape[1],), jnp.int32),
             pltpu.SemaphoreType.DMA((columns,)),
             pltpu.SemaphoreType.DMA((columns,)),
             pltpu.SemaphoreType.DMA,
@@ -502,18 +549,16 @@
             collective_id=1, has_side_effects=True, vmem_limit_bytes=40 << 20
         ),
         name="finish",
-    )(pages, queries, pre, done, acc, stat)
+    )(pages, docs, queries, pre, kv, done)
 
 
 def local(queries, kv_new, kv_pool, prefix_pages, reader_owner, send_page, tile_doc):
     columns, groups = lax.axis_size("ctx"), lax.axis_size("req")
-    rows = queries.shape[1]
     q, kv, pre, acc, stat = gather(
         send_page, reader_owner, prefix_pages, kv_pool, queries[0], kv_new[0], columns, groups, EARLY
     )
-    done, acc, stat = attend_new(tile_doc, q, kv, acc, stat, rows)
-    pre = pre.reshape(2, -1, HEAD)
-    return finish(prefix_pages, q, pre, done, acc, stat, columns)[None]
+    done = attend_new(tile_doc, q, kv, acc, stat, queries.shape[1])
+    return finish(prefix_pages, tile_doc, q, pre.reshape(2, -1, HEAD), kv, done, columns)[None]
 
 
 def solution(mesh):

time: 138 us -> 123 us (0.89)
  Pallas kernels: 130 us -> 119 us
  local copies, waits for them, and re-layouts: 6.48 us -> 1.33 us
    pallas_call x2, Pallas kernels: 59.7 us -> 50.1 us  [the longest x1 35.3 us: finish(): pl.pallas_call(lambda *refs: finish_kernel(columns, *refs), out_shape=jax...]
    unnamed x13 -> x3, local copies, waits for them, and re-layouts: 6.48 us -> 1.33 us
where the time goes in v4:
time: 123 us; the launch traced here: 121 us
  Pallas kernels  119 us (97%)
  local copies, waits for them, and re-layouts  1.33 us (1%)
    pallas_call x1, Pallas kernels, gather(): pl.pallas_call(lambda *refs: gather_kernel(columns, groups, early, *refs)...  69.3 us
    pallas_call x1, Pallas kernels, finish(): pl.pallas_call(lambda *refs: finish_kernel(columns, *refs), out_shape=jax...  35.3 us
    pallas_call x1, Pallas kernels, attend_new(): pl.pallas_call(lambda *refs: new_kernel(positions // rows, *refs), out_sh...  14.8 us

profile of v4, /device:TPU:10, one launch (start us, length us, event | category | flops | bytes accessed | tf_op | source)
XLA Modules:
  0.0 121.4 jit_solution(10872936359221213668)
XLA Ops:
  0.0 0.0 copy-start
  0.7 69.3 %gather.1 = (bf16[4096,256]{1,0:T(8,128)(2,1)S(1)}, bf16[2,4096,128]{2,1,0:T(8,128)(2,1)S(1)}, bf16[2,4,16,32,128]{4,3,2,1,0:T(8,128)(2,1)S(1)}, f32[2816,256]{1,0:T(8,128)S(1)}, f32[2816,128]{1,0:T(8,128)S(1)}) custom-call(s32[1,1,8]{2,1,0:T(1,128)} %refs_0_.3, s32[1,1,4]{2,1,0:T(1,128)} %refs_1_.2, s32[1]{0:T(128)S(6)} %copy.9.refs_2_.refs_0_, ...), custom_call_target="tpu_custom_call" | custom-call | tf_op jit(solution)/shard_map/gather/pallas_call | solution.py:366
  69.9 0.0 copy-done
  69.9 14.8 %attend_new.1.refs_5_ = bf16[2816,256]{1,0:T(8,128)(2,1)S(1)} custom-call(s32[1,32]{1,0:T(1,128)S(1)} %copy-done, bf16[4096,256]{1,0:T(8,128)(2,1)S(1)} %get-tuple-element.10.refs_1_.refs_2_, bf16[2,4096,128]{2,1,0:T(8,128)(2,1)S(1)} %get-tuple-element.12.refs_2_.refs_4_, f32[2816,256]{1,0:T(8,128)S(1)} %get-tuple-element.13.refs_3_, ...), custom_call_target="tpu_custom_call" | custom-call | tf_op jit(solution)/shard_map/attend_new/pallas_call | solution.py:448
  84.7 35.3 %finish.1 = bf16[256,4096]{1,0:T(8,128)(2,1)S(1)} custom-call(s32[1]{0:T(128)S(6)} %copy.9.refs_2_.refs_0_, s32[1,32]{1,0:T(1,128)S(1)} %copy-done, bf16[4096,256]{1,0:T(8,128)(2,1)S(1)} %get-tuple-element.10.refs_1_.refs_2_, bf16[2,2048,128]{2,1,0:T(8,128)(2,1)S(1)} %bitcast.5, bf16[2,4096,128]{2,1,0:T(8,128)(2,1)S(1)} %get-tuple-element.12.refs_2_.refs_4_, ...), custom_call_target="tpu_custom_call" | custom-call | tf_op jit(solution)/shard_map/finish/pallas_call | solution.py:536
  120.1 1.3 %copy.10 = bf16[1,256,4096]{2,1,0:T(8,128)(2,1)} copy(bf16[1,256,4096]{2,1,0:T(8,128)(2,1)S(1)} %bitcast.4) | data formatting | bytes 4194304
Async XLA Ops:
  0.0 69.9 %copy-start = (s32[1,32]{1,0:T(1,128)S(1)}, s32[1,32]{1,0:T(1,128)}, u32[]{:S(2)}) copy-start(s32[1,32]{1,0:T(1,128)} %refs_1_.3) | copy-start | bytes 388

commit v5 on v4

--- a/solution.py
+++ b/solution.py
@@ -92,13 +92,18 @@
     each(1, docs.shape[1], begin_of)
 
 
-def first_seen(starts, block, rows):
+def seen_by(starts, block, rows, start, size, causal):
     per = rows // TILE
-    row = lax.broadcasted_iota(jnp.int32, (rows, 1), 0)
-    low = jnp.full((rows, 1), starts[block * per] * TILE, jnp.int32)
-    for t in range(1, per):
-        low = jnp.where(row >= t * TILE, starts[block * per + t] * TILE, low)
-    return row, low
+    tiles = []
+    for t in range(per):
+        tile = block * per + t
+        column = lax.broadcasted_iota(jnp.int32, (TILE, size), 1)
+        seen = column >= starts[tile] * TILE - start
+        if causal:
+            row = lax.broadcasted_iota(jnp.int32, (TILE, size), 0)
+            seen = seen & (column - row <= tile * TILE - start)
+        tiles.append(seen)
+    return jnp.concatenate(tiles, axis=0)
 
 
 def joined(one, two):
@@ -107,19 +112,16 @@
     return top, one[1] * left + two[1] * right, one[2] * left + two[2] * right
 
 
-def pack(tops_and_totals):
-    shape = (tops_and_totals[0].shape[0], HEAD)
-    lane = lax.broadcasted_iota(jnp.int32, shape, 1)
-    stat = jnp.zeros(shape, jnp.float32)
-    for at, column in enumerate(tops_and_totals):
-        stat = jnp.where(lane == at, column, stat)
-    return stat
+def pack(columns):
+    return jnp.concatenate(
+        [jnp.broadcast_to(column, (column.shape[0], HEAD)) for column in columns], axis=1
+    )
 
 
 def part_of(acc_ref, stat_ref, at, h):
     return (
-        stat_ref[at, 2 * h : 2 * h + 1],
-        stat_ref[at, 2 * h + 1 : 2 * h + 2],
+        stat_ref[at, 2 * h * HEAD : (2 * h + 1) * HEAD],
+        stat_ref[at, (2 * h + 1) * HEAD : (2 * h + 2) * HEAD],
         acc_ref[at, h * HEAD : (h + 1) * HEAD],
     )
 
@@ -370,7 +372,7 @@
             jax.ShapeDtypeStruct((2, rows * columns, HEAD), dtype),
             jax.ShapeDtypeStruct((2, slots, columns, page_len, HEAD), dtype),
             jax.ShapeDtypeStruct((rows * early, width), jnp.float32),
-            jax.ShapeDtypeStruct((rows * early, HEAD), jnp.float32),
+            jax.ShapeDtypeStruct((rows * early, 2 * width), jnp.float32),
         ),
         in_specs=[hbm, hbm, smem, hbm, hbm, hbm],
         out_specs=(vmem, vmem, vmem, vmem, vmem),
@@ -406,23 +408,15 @@
     def do(slot):
         block = partner(me, slot, columns, False)
         begin = starts[block * per] // per
-        row, low = first_seen(starts, block, rows)
         at = span(block, rows)
 
         def fold(before):
-            def seen(start, size):
-                return lax.broadcasted_iota(jnp.int32, (rows, size), 1) + start >= low
-
-            def chunk(offset, size):
-                start = begin * rows + offset
-                return new_chunk(kv_ref, start, size, lambda: seen(start, size))
-
-            def last():
-                column = lax.broadcasted_iota(jnp.int32, (rows, rows), 1)
-                return seen(block * rows, rows) & (column <= row)
-
-            chunks = [chunk(*cut) for cut in cuts(before * rows)]
-            chunks.append(new_chunk(kv_ref, block * rows, rows, last))
+            def chunk(start, size, causal):
+                seen = lambda: seen_by(starts, block, rows, start, size, causal)
+                return new_chunk(kv_ref, start, size, seen)
+
+            chunks = [chunk(begin * rows + at, size, False) for at, size in cuts(before * rows)]
+            chunks.append(chunk(block * rows, rows, True))
             parts = attention(units_of(q_ref, at, heads), chunks)
             for h, part in enumerate(parts):
                 acc_s[:, h * HEAD : (h + 1) * HEAD] = part[2]
@@ -452,7 +446,7 @@
         out_specs=vmem,
         scratch_shapes=[
             pltpu.VMEM((rows, width), jnp.float32),
-            pltpu.VMEM((rows, HEAD), jnp.float32),
+            pltpu.VMEM((rows, 2 * width), jnp.float32),
             pltpu.SMEM((docs.shape[1],), jnp.int32),
         ],
         compiler_params=pltpu.CompilerParams(vmem_limit_bytes=40 << 20),
@@ -496,16 +490,11 @@
 
     def late(i):
         block = partner(me, early + i, columns, False)
-        row, low = first_seen(starts, block, rows)
         begin = jnp.maximum(block - longest, 0) * rows
 
         def chunk(offset, size):
             start = begin + offset
-
-            def seen():
-                column = lax.broadcasted_iota(jnp.int32, (rows, size), 1) + start
-                return (column >= low) & (column <= row + block * rows)
-
+            seen = lambda: seen_by(starts, block, rows, start, size, True)
             return new_chunk(kv_ref, start, size, seen)
 
         chunks = prefix_chunks(pre_ref, rows, live)

time: 123 us -> 120 us (0.976)
  Pallas kernels: 119 us -> 116 us
    pallas_call x1, Pallas kernels: 14.8 us -> 11.6 us  [attend_new(): pl.pallas_call(lambda *refs: new_kernel(positions // rows, *refs), out_sh...]
where the time goes in v5:
time: 120 us; the launch traced here: 118 us
  Pallas kernels  116 us (97%)
  local copies, waits for them, and re-layouts  1.33 us (1%)
    pallas_call x1, Pallas kernels, gather(): pl.pallas_call(lambda *refs: gather_kernel(columns, groups, early, *refs)...  69.2 us
    pallas_call x1, Pallas kernels, finish(): pl.pallas_call(lambda *refs: finish_kernel(columns, *refs), out_shape=jax...  35.4 us
    pallas_call x1, Pallas kernels, attend_new(): pl.pallas_call(lambda *refs: new_kernel(positions // rows, *refs), out_sh...  11.6 us

profile of v5, /device:TPU:10, one launch (start us, length us, event | category | flops | bytes accessed | tf_op | source)
XLA Modules:
  0.0 118.2 jit_solution(7691841457997518186)
XLA Ops:
  0.0 0.0 copy-start
  0.7 69.2 %gather.1 = (bf16[4096,256]{1,0:T(8,128)(2,1)S(1)}, bf16[2,4096,128]{2,1,0:T(8,128)(2,1)S(1)}, bf16[2,4,16,32,128]{4,3,2,1,0:T(8,128)(2,1)S(1)}, f32[2816,256]{1,0:T(8,128)S(1)}, f32[2816,512]{1,0:T(8,128)S(1)}) custom-call(s32[1,1,8]{2,1,0:T(1,128)} %refs_0_.3, s32[1,1,4]{2,1,0:T(1,128)} %refs_1_.2, s32[1]{0:T(128)S(6)} %copy.9.refs_2_.refs_0_, ...), custom_call_target="tpu_custom_call" | custom-call | tf_op jit(solution)/shard_map/gather/pallas_call | solution.py:368
  69.9 0.0 copy-done
  69.9 11.6 %attend_new.1.refs_5_ = bf16[2816,256]{1,0:T(8,128)(2,1)S(1)} custom-call(s32[1,32]{1,0:T(1,128)S(1)} %copy-done, bf16[4096,256]{1,0:T(8,128)(2,1)S(1)} %get-tuple-element.10.refs_1_.refs_2_, bf16[2,4096,128]{2,1,0:T(8,128)(2,1)S(1)} %get-tuple-element.12.refs_2_.refs_4_, f32[2816,256]{1,0:T(8,128)S(1)} %get-tuple-element.13.refs_3_, ...), custom_call_target="tpu_custom_call" | custom-call | tf_op jit(solution)/shard_map/attend_new/pallas_call | solution.py:442
  81.5 35.4 %finish.1 = bf16[256,4096]{1,0:T(8,128)(2,1)S(1)} custom-call(s32[1]{0:T(128)S(6)} %copy.9.refs_2_.refs_0_, s32[1,32]{1,0:T(1,128)S(1)} %copy-done, bf16[4096,256]{1,0:T(8,128)(2,1)S(1)} %get-tuple-element.10.refs_1_.refs_2_, bf16[2,2048,128]{2,1,0:T(8,128)(2,1)S(1)} %bitcast.5, bf16[2,4096,128]{2,1,0:T(8,128)(2,1)S(1)} %get-tuple-element.12.refs_2_.refs_4_, ...), custom_call_target="tpu_custom_call" | custom-call | tf_op jit(solution)/shard_map/finish/pallas_call | solution.py:525
  116.9 1.3 %copy.10 = bf16[1,256,4096]{2,1,0:T(8,128)(2,1)} copy(bf16[1,256,4096]{2,1,0:T(8,128)(2,1)S(1)} %bitcast.4) | data formatting | bytes 4194304
Async XLA Ops:
  0.0 69.9 %copy-start = (s32[1,32]{1,0:T(1,128)S(1)}, s32[1,32]{1,0:T(1,128)}, u32[]{:S(2)}) copy-start(s32[1,32]{1,0:T(1,128)} %refs_1_.3) | copy-start | bytes 388

commit v6 on v5

--- a/solution.py
+++ b/solution.py
@@ -286,9 +286,10 @@
     each(1, chips, lambda t: pre_copy(t).start())
     pre_twin.start()
     own[2].start()
-    each(first, columns, lambda r: q_copy(r).start())
+    each(first, early, lambda r: q_copy(r).start())
     each(1, chips, lambda t: kv_copy(t).start())
     kv_twin.start()
+    each(early, columns, lambda r: q_copy(r).start())
 
     def pre_relay(t):
         pre_onward(t).wait_recv()

time: 120 us -> 119 us (level)
  the two profiles are of different devices: /device:TPU:10 before, /device:TPU:35 now
where the time goes in v6:
time: 119 us; the launch traced here: 117 us
  Pallas kernels  115 us (97%)
  local copies, waits for them, and re-layouts  1.33 us (1%)
    pallas_call x1, Pallas kernels, gather(): pl.pallas_call(lambda *refs: gather_kernel(columns, groups, early, *refs)...  65 us
    pallas_call x1, Pallas kernels, finish(): pl.pallas_call(lambda *refs: finish_kernel(columns, *refs), out_shape=jax...  38 us
    pallas_call x1, Pallas kernels, attend_new(): pl.pallas_call(lambda *refs: new_kernel(positions // rows, *refs), out_sh...  12.4 us

profile of v6, /device:TPU:35, one launch (start us, length us, event | category | flops | bytes accessed | tf_op | source)
XLA Modules:
  0.0 117.4 jit_solution(17463299020949393853)
XLA Ops:
  0.0 0.0 copy-start
  0.7 65.0 %gather.1 = (bf16[4096,256]{1,0:T(8,128)(2,1)S(1)}, bf16[2,4096,128]{2,1,0:T(8,128)(2,1)S(1)}, bf16[2,4,16,32,128]{4,3,2,1,0:T(8,128)(2,1)S(1)}, f32[2816,256]{1,0:T(8,128)S(1)}, f32[2816,512]{1,0:T(8,128)S(1)}) custom-call(s32[1,1,8]{2,1,0:T(1,128)} %refs_0_.3, s32[1,1,4]{2,1,0:T(1,128)} %refs_1_.2, s32[1]{0:T(128)S(6)} %copy.9.refs_2_.refs_0_, ...), custom_call_target="tpu_custom_call" | custom-call | tf_op jit(solution)/shard_map/gather/pallas_call | solution.py:369
  65.6 0.0 copy-done
  65.6 12.4 %attend_new.1.refs_5_ = bf16[2816,256]{1,0:T(8,128)(2,1)S(1)} custom-call(s32[1,32]{1,0:T(1,128)S(1)} %copy-done, bf16[4096,256]{1,0:T(8,128)(2,1)S(1)} %get-tuple-element.10.refs_1_.refs_2_, bf16[2,4096,128]{2,1,0:T(8,128)(2,1)S(1)} %get-tuple-element.12.refs_2_.refs_4_, f32[2816,256]{1,0:T(8,128)S(1)} %get-tuple-element.13.refs_3_, ...), custom_call_target="tpu_custom_call" | custom-call | tf_op jit(solution)/shard_map/attend_new/pallas_call | solution.py:443
  78.1 38.0 %finish.1 = bf16[256,4096]{1,0:T(8,128)(2,1)S(1)} custom-call(s32[1]{0:T(128)S(6)} %copy.9.refs_2_.refs_0_, s32[1,32]{1,0:T(1,128)S(1)} %copy-done, bf16[4096,256]{1,0:T(8,128)(2,1)S(1)} %get-tuple-element.10.refs_1_.refs_2_, bf16[2,2048,128]{2,1,0:T(8,128)(2,1)S(1)} %bitcast.5, bf16[2,4096,128]{2,1,0:T(8,128)(2,1)S(1)} %get-tuple-element.12.refs_2_.refs_4_, ...), custom_call_target="tpu_custom_call" | custom-call | tf_op jit(solution)/shard_map/finish/pallas_call | solution.py:526
  116.1 1.3 %copy.10 = bf16[1,256,4096]{2,1,0:T(8,128)(2,1)} copy(bf16[1,256,4096]{2,1,0:T(8,128)(2,1)S(1)} %bitcast.4) | data formatting | bytes 4194304
Async XLA Ops:
  0.0 65.6 %copy-start = (s32[1,32]{1,0:T(1,128)S(1)}, s32[1,32]{1,0:T(1,128)}, u32[]{:S(2)}) copy-start(s32[1,32]{1,0:T(1,128)} %refs_1_.3) | copy-start | bytes 388
